TPU v7x, 256 devices: a whole 4x4x8 slice. The times are simulated.
256 devices in a mesh: cp: 8 (over x, z_hi), fsdp: 32 (over z_lo, y, core).
Axes of the slice: x: 4, y: 4, z: 8 (z_hi: 2, z_lo: 4; z = z_hi * 4 + z_lo), core: 2. Of those that a mesh axis runs over, the one named last changes fastest.
Arguments:
- hidden: bfloat16 [32, 1024, 16384], P('fsdp', 'cp'), may hold values from -6 to 6
- norm_gain: bfloat16 [16384], P('fsdp'), may hold values from 0.25 to 1.75
- query_weight: bfloat16 [16384, 256], P('fsdp'), may hold values from -0.0625 to 0.0625
- key_weight: bfloat16 [16384, 128], P('fsdp'), may hold values from -0.0625 to 0.0625
- value_weight: bfloat16 [16384, 128], P('fsdp'), may hold values from -0.046875 to 0.046875
- out_weight: bfloat16 [256, 16384], P(None, 'fsdp'), may hold values from -0.75 to 0.75
- doc_lengths: int32 [32, 4], P('fsdp'), may hold values from 1 to 512, 1024 in all within a row
Outputs:
- attention_out: bfloat16 [32, 1024, 16384], P('fsdp', 'cp')
Inputs may be any that keep to these rules, and one draw needn't show every extreme that they name: `doc_lengths`: each row holds the lengths of the 4 documents of one sequence in order; they sum to 1024 and the longest is exactly 512.
All inputs are finite; a program needn't handle non-finite values.
Results may differ from a plain program's by a relative error of at most 0.012.
Values may be sent and summed in bfloat16 or wider, within the bound.
A program may use at most 128 MiB of HBM per device.

v0:
```python
import math

import jax
import jax.numpy as jnp
from jax import lax
from jax.sharding import PartitionSpec as P

BLK = 128


EPSILON = 1e-05
THETA = 500000.0


def side_by_side(arrays, axis, dim, along):
    columns = [a.reshape(*a.shape[:along], -1) for a in arrays]
    both = jnp.concatenate(columns, axis=along)
    out, at, outs = (lax.all_gather(both, axis, axis=dim, tiled=True), 0, [])
    for a, column in zip(arrays, columns):
        section = out[..., at : at + column.shape[along]]
        outs.append(section.reshape(*section.shape[:along], *a.shape[along:]))
        at += column.shape[along]
    return tuple(outs)


def copy_for_each(array, axis):
    length = lax.axis_size(axis)
    return lax.all_to_all(
        jnp.broadcast_to(array[None], (length, *array.shape)), axis, 0, 0, tiled=True
    )


def laid_out(tiles, dim):
    tiles = jnp.moveaxis(tiles, 0, dim)
    shape = tiles.shape
    return tiles.reshape(*shape[:dim], shape[dim] * shape[dim + 1], *shape[dim + 2 :])


def gathered_copies(array, axis, dim):
    tiles = copy_for_each(array, axis)
    return laid_out(tiles, dim)


def side_by_side_2(arrays, axis, dim, along):
    ends, at = ([], 0)
    for a in arrays[:-1]:
        at += a.shape[along]
        ends.append(at)
    both = jnp.concatenate(arrays, axis=along)
    return tuple(jnp.split(gathered_copies(both, axis, dim), ends, axis=along))


def doc_tables(lengths, total):
    ends = jnp.cumsum(lengths)
    starts = ends - lengths
    places = jnp.arange(total, dtype=jnp.int32)
    after = (ends[None, :] <= places[:, None]).astype(jnp.int32)
    doc_ids = jnp.sum(after, axis=1)
    member = (doc_ids[:, None] == jnp.arange(lengths.shape[0], dtype=jnp.int32)[None, :]).astype(
        jnp.int32
    )
    offsets = places - jnp.sum(member * starts[None, :], axis=1)
    return (doc_ids, offsets)


def rotate(values, offsets):
    head_dim = values.shape[2]
    half = head_dim // 2
    rates = jnp.power(THETA, -2.0 * jnp.arange(half, dtype=jnp.float32) / head_dim)
    angles = offsets.astype(jnp.float32)[:, None] * rates[None, :]
    cosine = jnp.cos(angles)[:, None, :]
    sine = jnp.sin(angles)[:, None, :]
    first = values[:, :, :half]
    second = values[:, :, half:]
    return jnp.concatenate([first * cosine - second * sine, second * cosine + first * sine], axis=2)


def fold_panels(columns, pieces):
    gain_piece, query_piece, key_piece, value_piece = pieces
    normed = (columns * gain_piece.astype(jnp.float32)[None, :]).astype(jnp.bfloat16)
    return (
        jnp.dot(normed, query_piece, preferred_element_type=jnp.float32),
        jnp.dot(normed, key_piece, preferred_element_type=jnp.float32),
        jnp.dot(normed, value_piece, preferred_element_type=jnp.float32),
    )


def keep_same(operand):
    return operand


def attend_blocks(blocks, doc_ids, state, pieces):
    key_rows, value_rows = pieces
    count = key_rows.shape[0]
    tile_size = math.gcd(count, BLK)

    def one_tile(tile_index, inner):
        first = tile_index * tile_size
        key_tile = lax.dynamic_slice_in_dim(key_rows, tile_index * tile_size, tile_size, 0)
        value_tile = lax.dynamic_slice_in_dim(value_rows, tile_index * tile_size, tile_size, 0)
        key_places = first + jnp.arange(tile_size, dtype=jnp.int32)
        key_docs = lax.dynamic_slice_in_dim(doc_ids, first, tile_size, 0)
        updated = []
        for block, carried in zip(blocks, inner):
            queries, query_first = block
            length = queries.shape[1]
            query_docs = lax.dynamic_slice_in_dim(doc_ids, query_first, length, 0)
            query_places = query_first + jnp.arange(length, dtype=jnp.int32)
            live = jnp.logical_and(
                first <= query_first + length - 1, key_docs[tile_size - 1] >= query_docs[0]
            )

            def compute(operand):
                numer, denom = operand
                scores = jnp.einsum(
                    "hqd,kd->hqk", queries, key_tile, preferred_element_type=jnp.float32
                )
                allowed = jnp.logical_and(
                    query_docs[:, None] == key_docs[None, :],
                    key_places[None, :] <= query_places[:, None],
                )
                weights = jnp.where(allowed[None, :, :], jnp.exp(scores), jnp.float32(0.0))
                numer = numer + jnp.einsum(
                    "hqk,kd->hqd",
                    weights.astype(jnp.bfloat16),
                    value_tile,
                    preferred_element_type=jnp.float32,
                )
                return (numer, denom + jnp.sum(weights, axis=2))

            updated.append(lax.cond(live, compute, keep_same, carried))
        return tuple(updated)

    return lax.fori_loop(0, count // tile_size, one_tile, state)


def local(hidden, norm_gain, query_weight, key_weight, value_weight, out_weight, doc_lengths):
    rows = hidden.shape[1]
    head_dim = key_weight.shape[1]
    heads = query_weight.shape[1] // head_dim
    groups = lax.axis_size("cp")
    position = lax.axis_index("cp")
    doc_ids, offsets = doc_tables(doc_lengths[0], rows * groups)
    tokens = hidden[0].astype(jnp.float32)
    scaled = tokens * lax.rsqrt(jnp.mean(tokens * tokens, axis=1, keepdims=True) + EPSILON)
    query_raw, key_raw, value_raw = fold_panels(
        scaled, side_by_side((norm_gain, query_weight, key_weight, value_weight), "fsdp", 0, 1)
    )
    own_offsets = lax.dynamic_slice_in_dim(offsets, position * rows, rows, 0)
    queries = (
        rotate(query_raw.reshape(rows, heads, head_dim), own_offsets) * head_dim ** (-0.5)
    ).astype(jnp.bfloat16)
    queries = queries.transpose(1, 0, 2)
    key_rows = rotate(key_raw.reshape(rows, 1, head_dim), own_offsets)[:, 0, :].astype(jnp.bfloat16)
    value_rows = value_raw.astype(jnp.bfloat16)
    blocks = ((queries, position * rows),)
    start_state = tuple(
        (
            (
                jnp.zeros((heads, block[0].shape[1], head_dim), jnp.float32),
                jnp.zeros((heads, block[0].shape[1]), jnp.float32),
            )
            for block in blocks
        )
    )
    state = attend_blocks(
        blocks, doc_ids, start_state, side_by_side_2((key_rows, value_rows), "cp", 0, 1)
    )
    results = [
        (numer / denom[:, :, None])
        .astype(jnp.bfloat16)
        .transpose(1, 0, 2)
        .reshape(numer.shape[1], heads * head_dim)
        for numer, denom in state
    ]
    attended = results[0]
    mixed = jnp.dot(
        attended,
        lax.all_gather(out_weight, "fsdp", axis=1, tiled=True),
        preferred_element_type=jnp.float32,
    ).astype(jnp.bfloat16)
    return mixed[None, :, :]


def solution(mesh):
    in_specs = (
        P("fsdp", "cp", None),
        P("fsdp"),
        P("fsdp", None),
        P("fsdp", None),
        P("fsdp", None),
        P(None, "fsdp"),
        P("fsdp", None),
    )
    out_specs = P("fsdp", "cp", None)
    return jax.shard_map(local, mesh=mesh, in_specs=in_specs, out_specs=out_specs, check_vma=False)
```

profile of v0, /device:TPU:1, one launch (start us, length us, event | category | flops | bytes accessed | tf_op | source)
XLA Modules:
  0.0 229.7 jit_solution(12196940942636767293)
XLA Ops:
  6.5 0.8 reshape.223
  7.4 2.3 pad_maximum_fusion
  9.7 0.7 all-gather.5.cloned.1.call-update
  10.4 0.8 reduce-window.4
  11.4 0.7 fusion.48
  12.2 3.1 %fusion.12 = f32[128]{0:T(128)S(1)} fusion(bf16[1,128,16384]{2,1,0:T(8,128)(2,1)} %param.11), kind=kLoop, calls=%fused_computation.20 | loop fusion | flops 6291328 | bytes 4194816 | tf_op jit(solution)/shard_map/reduce_sum | solution.py:145
  15.3 0.2 multiply_cosine_fusion
  15.5 119.3 %all-gather.3.cloned.1.call-done = bf16[16384,513]{1,0:T(8,128)(2,1)} async-done(((bf16[512,513]{1,0:T(8,128)(2,1)}), bf16[16384,513]{1,0:T(8,128)(2,1)}) %all-gather.3.cloned.1.call-update) | async-done | bytes 16810000 | tf_op jit(solution)/shard_map/all_gather | solution.py:18
  134.9 3.0 %convert_reduce_fusion = f32[16384]{0:T(1024)S(1)} fusion(bf16[16384,513]{1,0:T(8,128)(2,1)} %all-gather.3.cloned.1.call-done), kind=kLoop, calls=%fused_computation.26 | loop fusion | flops 16384 | bytes 98304 | tf_op jit(solution)/shard_map/convert_element_type | solution.py:80
  137.9 8.3 %fusion.28 = f32[128,1,128]{0,2,1:T(8,128)S(1)} fusion(bf16[16384,513]{1,0:T(8,128)(2,1)} %all-gather.3.cloned.1.call-done, bf16[1,128,16384]{2,1,0:T(8,128)(2,1)} %param.11, f32[16384]{0:T(1024)S(1)} %convert_reduce_fusion, f32[128]{0:T(128)S(1)} %add_rsqrt_fusion), kind=kOutput, calls=%fused_computation.35 | convolution fusion | flops 545259520 | bytes 8520192 | tf_op jit(solution)/shard_map/dot_general | solution.py:83
  146.2 0.2 fusion.45
  146.5 7.2 %fusion.33 = bf16[128,128]{0,1:T(8,128)(2,1)S(1)} fusion(bf16[16384,513]{1,0:T(8,128)(2,1)} %all-gather.3.cloned.1.call-done, bf16[1,128,16384]{2,1,0:T(8,128)(2,1)S(1)} %copy-done, f32[16384]{0:T(1024)S(1)} %convert_reduce_fusion, f32[128]{0:T(128)S(1)} %add_rsqrt_fusion), kind=kOutput, calls=%fused_computation.36 | convolution fusion | flops 545275904 | bytes 8487424 | tf_op jit(solution)/shard_map/dot_general | solution.py:84
  153.8 0.8 broadcast_in_dim.23
  154.6 8.9 %all-to-all-start = ((bf16[8,128,256]{2,1,0:T(8,128)(2,1)}), bf16[8,128,256]{2,1,0:T(8,128)(2,1)S(1)}, u32[]{:S(2)}, u32[]{:S(2)}) async-start(bf16[8,128,256]{2,1,0:T(8,128)(2,1)} %broadcast_in_dim.23), calls=%async_computation | async-start | bytes 1048576 | tf_op jit(solution)/shard_map/all_to_all | solution.py:28
  163.5 9.9 %slice_bitcast_fusion = bf16[256,16384]{0,1:T(8,128)(2,1)} fusion(bf16[16384,513]{1,0:T(8,128)(2,1)} %all-gather.3.cloned.1.call-done), kind=kLoop, calls=%fused_computation.25 | loop fusion | bytes 16777216 | tf_op jit(solution)/shard_map/dot_general | solution.py:82
  173.4 12.0 %copy.21 = bf16[256,16384]{1,0:T(8,128)(2,1)} copy(bf16[256,16384]{0,1:T(8,128)(2,1)} %slice_bitcast_fusion) | data formatting | bytes 16777216 | tf_op jit(solution)/shard_map/dot_general | solution.py:82
  185.3 7.3 %fusion.18 = f32[128,2,128]{0,2,1:T(8,128)S(1)} fusion(bf16[2,128,16384]{2,1,0:T(8,128)(2,1)} %bitcast.68, bf16[1,128,16384]{2,1,0:T(8,128)(2,1)} %param.11, f32[16384]{0:T(1024)S(1)} %convert_reduce_fusion, f32[128]{0:T(128)S(1)} %add_rsqrt_fusion), kind=kOutput, calls=%fused_computation.28 | convolution fusion | flops 1082130432 | bytes 12780032 | tf_op jit(solution)/shard_map/dot_general | solution.py:82
  192.6 0.1 copy.22
  192.9 11.9 %while.17 = (s32[]{:T(128)}, f32[2,128,128]{2,1,0:T(8,128)S(1)}, f32[2,128]{1,0:T(2,128)S(1)}, s32[]{:T(128)}, s32[1024]{0:T(1024)S(1)}, /*index=5*/s32[128]{0:T...) while((s32[]{:T(128)}, f32[2,128,128]{2,1,0:T(8,128)S(1)}, ...), condition=%wide.region_8.9_spmd, body=%wide.region_4.8_spmd.sunk | while | flops 16957704 | bytes 567161 | solution.py:134
  193.0 0.6 slice.77
  194.2 0.6 conditional.2
  194.4 0.2 fusion.49
  194.6 0.2 convolution_add_fusion
  194.9 0.6 slice.77
  196.3 0.6 slice.77
  197.8 0.6 slice.77
  199.2 0.6 slice.77
  200.6 0.6 slice.77
  202.0 0.6 slice.77
  203.4 0.6 slice.77
  204.9 11.3 %all-gather.5.cloned.1.call-done = bf16[256,16384]{1,0:T(8,128)(2,1)} async-done(((bf16[256,512]{1,0:T(8,128)(2,1)}), bf16[256,16384]{1,0:T(8,128)(2,1)}) %all-gather.5.cloned.1.call-update) | async-done | bytes 8388624 | tf_op jit(solution)/shard_map/all_gather | solution.py:179
  216.2 6.7 %fusion.9 = bf16[1,128,16384]{2,1,0:T(8,128)(2,1)} fusion(bf16[128,256]{0,1:T(8,128)(2,1)S(1)} %bitcast.70, bf16[256,16384]{1,0:T(8,128)(2,1)} %all-gather.5.cloned.1.call-done), kind=kOutput, calls=%fused_computation.15 | convolution fusion | flops 1075838976 | bytes 12648448 | tf_op jit(solution)/shard_map/dot_general | solution.py:177
  (49 shorter events, 1.6 us)
Async XLA Ops:
  6.5 128.3 %all-gather.3.cloned.1.call-start = ((), (), s32[]{:S(2)}) async-start(), calls=%async_computation.1 | async-start | bytes 21626880 | tf_op jit(solution)/shard_map/all_gather | solution.py:18
  9.6 206.5 %all-gather.5.cloned.1.call-start = ((), (), s32[]{:S(2)}) async-start(), calls=%async_computation.2 | async-start | bytes 8650752 | tf_op jit(solution)/shard_map/all_gather | solution.py:179
  134.9 11.6 %copy-start = (bf16[1,128,16384]{2,1,0:T(8,128)(2,1)S(1)}, bf16[1,128,16384]{2,1,0:T(8,128)(2,1)}, u32[]{:S(2)}) copy-start(bf16[1,128,16384]{2,1,0:T(8,128)(2,1)} %param.11) | copy-start | bytes 12582916
  154.6 38.2 %all-to-all-start = ((bf16[8,128,256]{2,1,0:T(8,128)(2,1)}), bf16[8,128,256]{2,1,0:T(8,128)(2,1)S(1)}, u32[]{:S(2)}, u32[]{:S(2)}) async-start(bf16[8,128,256]{2,1,0:T(8,128)(2,1)} %broadcast_in_dim.23), calls=%async_computation | async-start | bytes 1048576 | tf_op jit(solution)/shard_map/all_to_all | solution.py:28
Sparse Core Ops, SparseCore 0:
  9.8 125.0 all-gather.2
  136.7 79.3 all-gather.4
where the time goes:
time: 230 us
  waiting for transfers between devices  131 us (57%)
  matrix products  29.8 us (13%)
  local copies, waits for them, and re-layouts  29.7 us (13%)
  between operations  13.6 us (6%)
  other arithmetic  10.7 us (5%)
  starting transfers between devices  8.9 us (4%)
  loops' own time  5.59 us (2%)
    all_gather x1, waiting for transfers between devices, side_by_side(): out, at, outs = (lax.all_gather(both, axis, axis=dim, tiled=True), 0, [])  119 us
    dot_general x2, local copies, waits for them, and re-layouts, fold_panels(): jnp.dot(normed, query_piece, preferred_element_type=jnp.float32)  21.9 us
    all_gather x1, waiting for transfers between devices, local(): lax.all_gather(out_weight, 'fsdp', axis=1, tiled=True)  11.3 us
    all_to_all x1, starting transfers between devices, copy_for_each(): lax.all_to_all(jnp.broadcast_to(array[None], (length, *array.shape)), axi...  8.86 us
    dot_general x1, matrix products, fold_panels(): jnp.dot(normed, key_piece, preferred_element_type=jnp.float32)  8.33 us
    dot_general x1, matrix products, fold_panels(): jnp.dot(normed, query_piece, preferred_element_type=jnp.float32)  7.26 us
    dot_general x1, matrix products, fold_panels(): jnp.dot(normed, value_piece, preferred_element_type=jnp.float32)  7.16 us
    dot_general x1, matrix products, local(): jnp.dot(attended, lax.all_gather(out_weight, 'fsdp', axis=1, tiled=True),...  6.69 us
  transfers between devices with their start and end apart: 3, of which 2 were waited for; matrix products, arithmetic and copies ran while one was open for 26% of the time, Pallas kernels for 0%

commit v1 on v0

v1 whole, which is shorter than its diff:
```python
import jax
import jax.numpy as jnp
import numpy as np
from jax import lax
from jax.experimental import pallas as pl
from jax.experimental.pallas import tpu as pltpu
from jax.sharding import PartitionSpec as P

MESH = pl.DeviceIdType.MESH
EPSILON = 1e-05
THETA = 500000.0

ROWS = 128
D = 16384
SHARD = 512
HD = 128
NS = 16
BF = jnp.bfloat16
F32 = jnp.float32

SLOTS = [(0, 0), (3, 0), (1, 0), (0, 3), (0, 1), (3, 3), (1, 3), (3, 1), (1, 1), (2, 0), (0, 2), (2, 3), (2, 1), (3, 2),
         (1, 2), (2, 2)]
SLOT = {o: i for i, o in enumerate(SLOTS)}

ORDER = [(0, (3, 0)), (0, (1, 0)), (1, (0, 3)), (1, (0, 1)), (0, (0, 3)), (0, (0, 1)), (1, (3, 0)), (1, (1, 0)),
         (0, (2, 0)), (1, (0, 2)), (0, (3, 3)), (0, (3, 1)), (1, (3, 3)), (1, (1, 3)), (0, (1, 3)), (0, (1, 1)),
         (1, (3, 1)), (1, (1, 1)), (0, (0, 2)), (1, (2, 0)), (1, (2, 3)), (0, (2, 3)), (0, (2, 1)), (1, (2, 1)),
         (0, (3, 2)), (1, (3, 2)), (0, (1, 2)), (1, (1, 2)), (0, (2, 2)), (1, (2, 2))]


def forwards(half, offset):
    p, q = offset if half == 0 else offset[::-1]
    first, second = ("y", "z") if half == 0 else ("z", "y")
    put = (lambda a, b: (a, b)) if half == 0 else (lambda a, b: (b, a))
    out = []
    if q == 0:
        if p == 0:
            out += [(first + "+", put(3, 0), None), (first + "-", put(1, 0), None)]
        if p == 3:
            out += [(first + "+", put(2, 0), 0)]
        if p == 1:
            out += [(first + "-", put(2, 0), 1)]
        out += [(second + "+", put(p, 3), None), (second + "-", put(p, 1), None)]
    if q == 3:
        out += [(second + "+", put(p, 2), 0)]
    if q == 1:
        out += [(second + "-", put(p, 2), 1)]
    return out


def device(x, y, z, c):
    x, y, z = lax.rem(x + 4, 4), lax.rem(y + 4, 4), lax.rem(z + 8, 8)
    return (x * 2 + z // 4, ((lax.rem(z, 4) * 4) + y) * 2 + c)


def kernel(hid, gain_ref, wq, wk, wv, wo, dl_ref, rates_ref, out,
           hown, wraw, wbuf, xbuf, acc, srx, ptx, prx, kvbuf, wobuf, outv, qbuf, att,
           lsem, hsem, wsem, osem, dsem, ssem, psem, ksem, outsem, send, ksend):
    cp, fs = lax.axis_index("cp"), lax.axis_index("fsdp")
    x, zh = cp // 2, lax.rem(cp, 2)
    c = lax.rem(fs, 2)
    y = lax.rem(fs // 2, 4)
    zl = fs // 8
    z = zh * 4 + zl
    par = lax.rem(x, 2)
    other = 1 - c

    half = pl.multiple_of(par * 256, 256)
    own_w = [
        pltpu.make_async_copy(wq.at[pl.ds(half, 256)], wraw.at[:, pl.ds(0, 256)], lsem.at[0]),
        pltpu.make_async_copy(wk.at[pl.ds(half, 256)], wraw.at[:, pl.ds(256, 128)], lsem.at[1]),
        pltpu.make_async_copy(wv.at[pl.ds(half, 256)], wraw.at[:, pl.ds(384, 128)], lsem.at[2]),
    ]
    own_h = pltpu.make_async_copy(hid, hown, lsem.at[3])
    own_o = pltpu.make_async_copy(wo, wobuf.at[0, 0], lsem.at[4])
    for copy in own_w:
        copy.start()
    own_h.start()
    own_o.start()

    sibling = device(x, y, z, other)
    step_a = 1 - 2 * par
    partners = [(x + step_a), (x - step_a)]
    link = {"y+": device(x, y + 1, z, c), "y-": device(x, y - 1, z, c),
            "z+": device(x, y, z + 1, c), "z-": device(x, y, z - 1, c)}

    barrier = pltpu.get_barrier_semaphore()
    peers = list(link.values()) + [sibling] + [device(p, y, z, other) for p in partners]
    peers += [(lax.rem(cp + d, 8), fs) for d in range(1, 8)]
    for peer in peers:
        pl.semaphore_signal(barrier, inc=1, device_id=peer, device_id_type=MESH)
    pl.semaphore_wait(barrier, len(peers))

    def column(slot, core):
        dy, dz = SLOTS[slot]
        return ((lax.rem(zl + dz, 4) * 4 + lax.rem(y + dy, 4)) * 2 + core) * SHARD

    def send_hidden(pair):
        for s in (2 * pair, 2 * pair + 1):
            for p in range(2):
                plans = [(sibling, 0, other, par), (device(partners[p], y, z, c), 1, c, 1 - par),
                         (device(partners[p], y, z, other), 2, other, 1 - par)]
                for dst, block, core, parity in plans:
                    col = pl.multiple_of(column(s, core) + (parity * 2 + p) * 128, 128)
                    pltpu.make_async_remote_copy(
                        src_ref=hid.at[:, pl.ds(col, 128)],
                        dst_ref=xbuf.at[p, pl.ds(block * 128, 128), pl.ds(s * 128, 128)],
                        send_sem=send.at[0], recv_sem=hsem.at[p, pair], device_id=dst, device_id_type=MESH).start()

    def wait_hidden(p, pair):
        ref = xbuf.at[p, :, pl.ds(pair * 256, 256)]
        pltpu.make_async_copy(ref, ref, hsem.at[p, pair]).wait()

    def w_view(h, slot, part):
        rows, cols = pl.ds(slot * 128, 128), pl.ds(h * 256, 256)
        return wbuf.at[:, rows, cols] if part is None else wbuf.at[part, rows, cols]

    def o_view(h, slot, part):
        rows = pl.ds(0, 256) if part is None else pl.ds(part * 128, 128)
        return wobuf.at[0, slot, rows, pl.ds(h * 256, 256)]

    def relay(view, sem, which, h, offset):
        for name, there, part in forwards(h, offset):
            pltpu.make_async_remote_copy(
                src_ref=view(h, SLOT[offset], part), dst_ref=view(h, SLOT[there], part),
                send_sem=send.at[which], recv_sem=sem.at[h, SLOT[there]],
                device_id=link[name], device_id_type=MESH).start()

    def arrive(view, sem, h, offset):
        ref = view(h, SLOT[offset], None)
        pltpu.make_async_copy(ref, ref, sem.at[h, SLOT[offset]]).wait()

    send_hidden(0)

    for copy in own_w:
        copy.wait()
    gains = gain_ref[...]
    gains = jnp.where(par == 0, gains[:, :256].astype(F32), gains[:, 256:].astype(F32))
    row = lax.broadcasted_iota(jnp.int32, (256, 256), 0)
    col = lax.broadcasted_iota(jnp.int32, (256, 256), 1)
    diagonal = jnp.where(row == col, jnp.broadcast_to(gains, (256, 256)), 0.0).astype(BF)
    scaled = jnp.dot(diagonal, wraw[...], preferred_element_type=F32).astype(BF)
    wbuf[0, 0:128, :] = scaled[:128]
    wbuf[1, 0:128, :] = scaled[128:]
    relay(w_view, wsem, 1, 0, (0, 0))
    relay(w_view, wsem, 1, 1, (0, 0))
    for pair in range(1, 8):
        send_hidden(pair)

    own_h.wait()

    def square(i, total):
        block = hown[:, pl.ds(pl.multiple_of(i * 512, 512), 512)].astype(F32)
        sq = block * block
        return total + (sq[:, :128] + sq[:, 128:256]) + (sq[:, 256:384] + sq[:, 384:])

    total = lax.fori_loop(0, D // 512, square, jnp.zeros((ROWS, 128), F32))
    scale = lax.rsqrt(jnp.sum(total, axis=1, keepdims=True) * (1.0 / D) + EPSILON)
    places = lax.broadcasted_iota(jnp.int32, (ROWS, 128), 0) + cp * ROWS
    starts = jnp.zeros((ROWS, 128), jnp.int32)
    end = dl_ref[0, 0]
    for j in range(1, 4):
        starts = jnp.where(places >= end, end, starts)
        end = end + dl_ref[0, j]
    angles = (places - starts).astype(F32) * rates_ref[...]
    cosine = jnp.cos(angles)
    sine = jnp.sin(angles)
    lane = lax.broadcasted_iota(jnp.int32, (ROWS, 128), 1)
    sine = jnp.where(lane < 64, -sine, sine)

    def rotate(u):
        return u * cosine + pltpu.roll(u, 64, axis=1) * sine

    def contract(pair):
        for p in range(2):
            wait_hidden(p, pair)
            own = []
            for s in (2 * pair, 2 * pair + 1):
                at = pl.multiple_of(column(s, c) + (par * 2 + p) * 128, 128)
                own.append(hown[:, pl.ds(at, 128)])
            weights = wbuf[p, pair * 256:(pair + 1) * 256, :]
            lhs = jnp.concatenate([jnp.concatenate(own, axis=1), xbuf[p, :, pair * 256:(pair + 1) * 256]], axis=0)
            r = jnp.dot(lhs, weights, preferred_element_type=F32)
            for block, at in enumerate((0, 3, 1 + p, 4 + p)):
                piece = r[block * 128:(block + 1) * 128]
                fresh = pair == 0 and (p == 0 or block >= 2)
                acc[at] = piece if fresh else acc[at] + piece

    seen = {(0, (0, 0)), (1, (0, 0))}
    done = 0
    last = max(i for i, (h, o) in enumerate(ORDER) if forwards(h, o))
    for i, (h, o) in enumerate(ORDER):
        arrive(w_view, wsem, h, o)
        relay(w_view, wsem, 1, h, o)
        seen.add((h, o))
        if i == last:
            own_o.wait()
            relay(o_view, osem, 2, 0, (0, 0))
            relay(o_view, osem, 2, 1, (0, 0))
        while done < 8 and all((k, SLOTS[2 * done + e]) in seen for k in range(2) for e in range(2)):
            contract(done)
            done += 1

    def across(slot):
        return pltpu.make_async_remote_copy(
            src_ref=wobuf.at[0, slot], dst_ref=wobuf.at[1, slot], send_sem=send.at[3], recv_sem=dsem.at[slot],
            device_id=sibling, device_id_type=MESH)

    o_seen = {(0, (0, 0)), (1, (0, 0))}

    def take_out(count):
        for h, o in ORDER[len(o_seen) - 2:len(o_seen) - 2 + count]:
            arrive(o_view, osem, h, o)
            relay(o_view, osem, 2, h, o)
            o_seen.add((h, o))
            if (1 - h, o) in o_seen:
                across(SLOT[o]).start()

    to_sibling = pltpu.make_async_remote_copy(
        src_ref=acc.at[pl.ds(3, 3)], dst_ref=srx, send_sem=send.at[4], recv_sem=ssem,
        device_id=sibling, device_id_type=MESH)
    to_sibling.start()
    across(0).start()
    to_sibling.wait_recv()
    for part, cols in ((1, slice(256, 512)), (0, slice(0, 256))):
        for p in range(2):
            ptx[part, p] = (acc[1 + p, :, cols] + srx[1 + p, :, cols]).astype(BF)
            pltpu.make_async_remote_copy(
                src_ref=ptx.at[part, p], dst_ref=prx.at[part, p], send_sem=send.at[5], recv_sem=psem.at[part, p],
                device_id=device(partners[p], y, z, c), device_id_type=MESH).start()

    def finish(part, cols):
        value = acc[0, :, cols] + srx[0, :, cols]
        for p in range(2):
            ref = prx.at[part, p]
            pltpu.make_async_copy(ref, ref, psem.at[part, p]).wait()
            value = value + prx[part, p].astype(F32)
        return value * scale

    kv = finish(1, slice(256, 512))
    kvbuf[512:640, 0:128] = rotate(kv[:, :128]).astype(BF)
    kvbuf[512:640, 128:256] = kv[:, 128:].astype(BF)

    def kv_copy(d):
        return pltpu.make_async_remote_copy(
            src_ref=kvbuf.at[pl.ds(512, 128)], dst_ref=kvbuf.at[pl.ds((4 - d) * ROWS, ROWS)], send_sem=ksend.at[d - 1], recv_sem=ksem.at[d - 1],
            device_id=(lax.rem(cp + d, 8), fs), device_id_type=MESH)

    for d in (1, 3, 2, 4):
        pl.when(cp + d < 8)(kv_copy(d).start)
    take_out(2)

    qs = finish(0, slice(0, 256))
    qbuf[0:128, :] = (rotate(qs[:, :128]) * HD ** -0.5).astype(BF)
    qbuf[128:256, :] = (rotate(qs[:, 128:]) * HD ** -0.5).astype(BF)
    take_out(2)
    for d in (2, 4, 1, 3):
        @pl.when(cp >= d)
        def _():
            kv_copy(d).wait_recv()

        @pl.when(cp < d)
        def _():
            kvbuf[(4 - d) * ROWS:(5 - d) * ROWS, :] = jnp.zeros((ROWS, 256), BF)

    scores = lax.dot_general(qbuf[...], kvbuf[:, :128], (((1,), (1,)), ((), ())), preferred_element_type=F32)
    keys = lax.broadcasted_iota(jnp.int32, (ROWS, 5 * ROWS), 1) + (cp - 4) * ROWS
    allowed = (keys >= starts[:, :1]) & (keys <= places[:, :1])
    e = jnp.where(jnp.concatenate([allowed, allowed], axis=0), jnp.exp(scores), 0.0)
    mixed = jnp.dot(e.astype(BF), kvbuf[:, 128:], preferred_element_type=F32) / jnp.sum(e, axis=1, keepdims=True)
    att[:, 0:128] = mixed[:128].astype(BF)
    att[:, 128:256] = mixed[128:].astype(BF)

    def project(which, slot, core):
        o = jnp.dot(att[...], wobuf[which, slot], preferred_element_type=F32).astype(BF)
        outv[which, slot] = o
        at = pl.multiple_of(column(slot, core), SHARD)
        pltpu.make_async_copy(outv.at[which, slot], out.at[:, pl.ds(at, SHARD)], outsem).start()

    def sibling_out(slot):
        ref = wobuf.at[1, slot]
        pltpu.make_async_copy(ref, ref, dsem.at[slot]).wait()
        project(1, slot, other)

    ready = [s for s in range(NS) if (0, SLOTS[s]) in o_seen and (1, SLOTS[s]) in o_seen]
    projected = set()
    pending = []
    for s in ready:
        project(0, s, c)
        projected.add(s)
        pending.append(s)
    while len(o_seen) < 32:
        take_out(1)
        for s in range(NS):
            if s not in projected and (0, SLOTS[s]) in o_seen and (1, SLOTS[s]) in o_seen:
                project(0, s, c)
                projected.add(s)
                pending.append(s)
        if len(pending) > 2:
            sibling_out(pending.pop(0))
    for s in pending:
        sibling_out(s)

    def drain(ref, sem):
        pltpu.make_async_copy(ref, ref, sem).wait()

    drain(xbuf, send.at[0])
    drain(wbuf.at[:, pl.ds(128, 15 * 128)], send.at[1])
    drain(wobuf.at[0, pl.ds(1, 15)], send.at[2])
    drain(wobuf.at[1], send.at[3])
    drain(srx, send.at[4])
    drain(prx, send.at[5])
    for d in (1, 2, 3, 4):
        pl.when(cp + d < 8)(kv_copy(d).wait_send)
    drain(outv, outsem)


def local(hidden, norm_gain, query_weight, key_weight, value_weight, out_weight, doc_lengths):
    rates = np.power(np.float32(THETA), -2.0 * np.arange(64, dtype=np.float32) / np.float32(128.0)).astype(np.float32)
    rates = jnp.asarray(np.concatenate([rates, rates])[None, :])
    anywhere = pl.BlockSpec(memory_space=pl.ANY)
    vmem = pl.BlockSpec(memory_space=pltpu.VMEM)
    dma = pltpu.SemaphoreType.DMA
    out = pl.pallas_call(
        kernel,
        out_shape=jax.ShapeDtypeStruct((ROWS, D), BF),
        in_specs=[anywhere, vmem, anywhere, anywhere, anywhere, anywhere,
                  pl.BlockSpec(memory_space=pltpu.SMEM), vmem],
        out_specs=anywhere,
        scratch_shapes=[
            pltpu.VMEM((ROWS, D), BF),
            pltpu.VMEM((256, 512), BF),
            pltpu.VMEM((2, NS * 128, 512), BF),
            pltpu.VMEM((2, 384, NS * 128), BF),
            pltpu.VMEM((6, ROWS, 512), F32),
            pltpu.VMEM((3, ROWS, 512), F32),
            pltpu.VMEM((2, 2, ROWS, 256), BF),
            pltpu.VMEM((2, 2, ROWS, 256), BF),
            pltpu.VMEM((5 * ROWS, 256), BF),
            pltpu.VMEM((2, NS, 256, 512), BF),
            pltpu.VMEM((2, NS, ROWS, 512), BF),
            pltpu.VMEM((2 * ROWS, HD), BF),
            pltpu.VMEM((ROWS, 256), BF),
            dma((5,)), dma((2, 8)), dma((2, NS)), dma((2, NS)), dma((NS,)), dma, dma((2, 2)), dma((4,)), dma,
            dma((6,)), dma((4,)),
        ],
        compiler_params=pltpu.CompilerParams(collective_id=0, has_side_effects=True, vmem_limit_bytes=48 << 20),
    )(hidden[0], norm_gain[None, :], query_weight, key_weight, value_weight, out_weight, doc_lengths, rates)
    return out[None]


def solution(mesh):
    in_specs = (
        P("fsdp", "cp", None),
        P("fsdp"),
        P("fsdp", None),
        P("fsdp", None),
        P("fsdp", None),
        P(None, "fsdp"),
        P("fsdp", None),
    )
    out_specs = P("fsdp", "cp", None)
    return jax.shard_map(local, mesh=mesh, in_specs=in_specs, out_specs=out_specs, check_vma=False)
```

time: 230 us -> 82.8 us (0.36)
  waiting for transfers between devices: 131 us -> 0 us
  Pallas kernels: 0 us -> 74.9 us
  matrix products: 29.8 us -> 0 us
  local copies, waits for them, and re-layouts: 29.7 us -> 7.71 us
  between operations: 13.6 us -> 0.02 us
  other arithmetic: 10.7 us -> 0 us
  starting transfers between devices: 8.9 us -> 0 us
  loops' own time: 5.59 us -> 0 us
    all_gather x2 -> x0, waiting for transfers between devices: 131 us -> none  [the longest x1 119 us: side_by_side(): out, at, outs = (lax.all_gather(both, axis, axis=dim, tiled=True), 0, [])]
    pallas_call x0 -> x1, Pallas kernels: none -> 74.9 us  [local(): pl.pallas_call(kernel, out_shape=jax.ShapeDtypeStruct((ROWS, D), BF), in_...]
    dot_general x6 -> x0, matrix products: 29.8 us -> none  [the longest x1 8.33 us: fold_panels(): jnp.dot(normed, key_piece, preferred_element_type=jnp.float32)]
    dot_general x2 -> x0, local copies, waits for them, and re-layouts: 21.9 us -> none  [fold_panels(): jnp.dot(normed, query_piece, preferred_element_type=jnp.float32)]
    all_to_all x1 -> x0, starting transfers between devices: 8.86 us -> none  [copy_for_each(): lax.all_to_all(jnp.broadcast_to(array[None], (length, *array.shape)), axi...]
    unnamed x2 -> x13, local copies, waits for them, and re-layouts: 0.01 us -> 7.03 us
    another operation x9 -> x0, loops' own time: 5.59 us -> none  [the longest x1 5.43 us: attend_blocks(): return lax.fori_loop(0, count // tile_size, one_tile, state)]
    slice x8 -> x0, local copies, waits for them, and re-layouts: 5.16 us -> none  [one_tile(): key_docs[tile_size - 1] >= query_docs[0]]
  transfers between devices with their start and end apart: 3 -> 0, of which waited for: 2 -> 0; matrix products, arithmetic and copies ran while one was open for 26% -> 0% of each run, Pallas kernels for 0% -> 0%
where the time goes in v1:
time: 82.8 us; the launch traced here: 82.6 us
  Pallas kernels  74.9 us (90%)
  local copies, waits for them, and re-layouts  7.71 us (9%)
    pallas_call x1, Pallas kernels, local(): pl.pallas_call(kernel, out_shape=jax.ShapeDtypeStruct((ROWS, D), BF), in_...  74.9 us
    unnamed x13, local copies, waits for them, and re-layouts  7.03 us

profile of v1, /device:TPU:1, one launch (start us, length us, event | category | flops | bytes accessed | tf_op | source)
XLA Modules:
  0.0 82.6 jit_solution(10608609907260103303)
XLA Ops:
  0.0 0.7 broadcast_in_dim.6.gain_ref
  0.7 0.0 copy-start
  0.7 0.9 %copy-done = bf16[512,256]{1,0:T(8,128)(2,1)S(1)} copy-done((bf16[512,256]{1,0:T(8,128)(2,1)S(1)}, bf16[512,256]{1,0:T(8,128)(2,1)}, u32[]{:S(2)}) %copy-start) | copy-done | bytes 262168
  1.6 0.0 copy-start.1
  1.6 0.9 %copy-done.1 = bf16[256,512]{1,0:T(8,128)(2,1)S(1)} copy-done((bf16[256,512]{1,0:T(8,128)(2,1)S(1)}, bf16[256,512]{1,0:T(8,128)(2,1)}, u32[]{:S(2)}) %copy-start.1) | copy-done | bytes 262168
  2.6 0.0 copy-start.2
  2.6 0.9 %copy-done.2 = bf16[512,128]{1,0:T(8,128)(2,1)S(1)} copy-done((bf16[512,128]{1,0:T(8,128)(2,1)S(1)}, bf16[512,128]{1,0:T(8,128)(2,1)}, u32[]{:S(2)}) %copy-start.2) | copy-done | bytes 131096
  3.5 0.0 copy-start.3
  3.5 0.9 %copy-done.3 = bf16[512,128]{1,0:T(8,128)(2,1)S(1)} copy-done((bf16[512,128]{1,0:T(8,128)(2,1)S(1)}, bf16[512,128]{1,0:T(8,128)(2,1)}, u32[]{:S(2)}) %copy-start.3) | copy-done | bytes 131096
  4.4 0.0 copy-start.4
  4.4 0.7 copy-done.4
  5.0 0.0 copy-start.5
  5.1 0.7 copy-done.5
  5.7 74.9 %shard_map.82 = bf16[128,16384]{1,0:T(8,128)(2,1)S(1)} custom-call(bf16[128,16384]{1,0:T(8,128)(2,1)} %bitcast.3, bf16[1,512]{1,0:T(2,128)(2,1)S(1)} %broadcast_in_dim.6.gain_ref, bf16[512,256]{1,0:T(8,128)(2,1)S(1)} %copy-done, bf16[512,128]{1,0:T(8,128)(2,1)S(1)} %copy-done.2, bf16[512,128]{1,0:T(8,128)(2,1)S(1)} %copy-done.3, ...), custom_call_target="tpu_custom_call" | custom-call | tf_op jit(solution)/shard_map/pallas_call | solution.py:324
  80.6 2.0 %copy.10 = bf16[1,128,16384]{2,1,0:T(8,128)(2,1)} copy(bf16[1,128,16384]{2,1,0:T(8,128)(2,1)S(1)} %bitcast.2) | data formatting | bytes 8388608
Async XLA Ops:
  0.7 0.9 %copy-start = (bf16[512,256]{1,0:T(8,128)(2,1)S(1)}, bf16[512,256]{1,0:T(8,128)(2,1)}, u32[]{:S(2)}) copy-start(bf16[512,256]{1,0:T(8,128)(2,1)} %wq.1) | copy-start | bytes 786436
  1.6 0.9 %copy-start.1 = (bf16[256,512]{1,0:T(8,128)(2,1)S(1)}, bf16[256,512]{1,0:T(8,128)(2,1)}, u32[]{:S(2)}) copy-start(bf16[256,512]{1,0:T(8,128)(2,1)} %wo.1) | copy-start | bytes 786436
  2.6 0.9 %copy-start.2 = (bf16[512,128]{1,0:T(8,128)(2,1)S(1)}, bf16[512,128]{1,0:T(8,128)(2,1)}, u32[]{:S(2)}) copy-start(bf16[512,128]{1,0:T(8,128)(2,1)} %wk.1) | copy-start | bytes 393220
  3.5 0.9 %copy-start.3 = (bf16[512,128]{1,0:T(8,128)(2,1)S(1)}, bf16[512,128]{1,0:T(8,128)(2,1)}, u32[]{:S(2)}) copy-start(bf16[512,128]{1,0:T(8,128)(2,1)} %wv.1) | copy-start | bytes 393220
  4.4 0.7 copy-start.4
  5.0 0.7 copy-start.5

commit v2 on v1

--- a/solution.py
+++ b/solution.py
@@ -18,14 +18,16 @@
 BF = jnp.bfloat16
 F32 = jnp.float32
 
-SLOTS = [(0, 0), (3, 0), (1, 0), (0, 3), (0, 1), (3, 3), (1, 3), (3, 1), (1, 1), (2, 0), (0, 2), (2, 3), (2, 1), (3, 2),
-         (1, 2), (2, 2)]
+SLOTS = [(0, 0), (1, 0), (3, 0), (0, 3), (3, 3), (1, 1), (1, 3), (0, 1), (3, 1), (2, 3), (2, 1), (1, 2), (3, 2), (0, 2),
+         (2, 0), (2, 2)]
 SLOT = {o: i for i, o in enumerate(SLOTS)}
 
-ORDER = [(0, (3, 0)), (0, (1, 0)), (1, (0, 3)), (1, (0, 1)), (0, (0, 3)), (0, (0, 1)), (1, (3, 0)), (1, (1, 0)),
-         (0, (2, 0)), (1, (0, 2)), (0, (3, 3)), (0, (3, 1)), (1, (3, 3)), (1, (1, 3)), (0, (1, 3)), (0, (1, 1)),
-         (1, (3, 1)), (1, (1, 1)), (0, (0, 2)), (1, (2, 0)), (1, (2, 3)), (0, (2, 3)), (0, (2, 1)), (1, (2, 1)),
-         (0, (3, 2)), (1, (3, 2)), (0, (1, 2)), (1, (1, 2)), (0, (2, 2)), (1, (2, 2))]
+ORDER = [(0, (1, 0)), (1, (0, 3)), (0, (3, 0)), (1, (1, 0)), (1, (0, 1)), (1, (3, 3)), (1, (1, 3)), (1, (3, 0)),
+         (0, (2, 0)), (0, (1, 1)), (1, (0, 2)), (0, (0, 3)), (0, (3, 3)), (1, (1, 1)), (0, (3, 1)), (0, (1, 3)),
+         (0, (0, 1)), (0, (2, 3)), (0, (2, 1)), (1, (3, 1)), (1, (2, 3)), (1, (3, 2)), (1, (1, 2)), (1, (2, 1)),
+         (0, (1, 2)), (0, (3, 2)), (0, (0, 2)), (1, (2, 0)), (1, (2, 2)), (0, (2, 2))]
+OPENING = ((0, "y"), (1, "z"), (0, "z"), (1, "y"))
+TAKE = (3, 2, 1, 6)
 
 
 def forwards(half, offset):
@@ -53,9 +55,9 @@
     return (x * 2 + z // 4, ((lax.rem(z, 4) * 4) + y) * 2 + c)
 
 
-def kernel(hid, gain_ref, wq, wk, wv, wo, dl_ref, rates_ref, out,
-           hown, wraw, wbuf, xbuf, acc, srx, ptx, prx, kvbuf, wobuf, outv, qbuf, att,
-           lsem, hsem, wsem, osem, dsem, ssem, psem, ksem, outsem, send, ksend):
+def kernel(hid, gain_hbm, wq, wk, wv, wo, dl_hbm, rates_hbm, out,
+           gain_ref, dl_ref, rates_ref, hown, wraw, wbuf, xbuf, acc, srx, ptx, prx, kvbuf, wobuf, qbuf, att,
+           lsem, hsem, wsem, osem, dsem, ssem, psem, ksem, send, ksend):
     cp, fs = lax.axis_index("cp"), lax.axis_index("fsdp")
     x, zh = cp // 2, lax.rem(cp, 2)
     c = lax.rem(fs, 2)
@@ -75,6 +77,10 @@
     own_o = pltpu.make_async_copy(wo, wobuf.at[0, 0], lsem.at[4])
     for copy in own_w:
         copy.start()
+    small = [pltpu.make_async_copy(gain_hbm, gain_ref, lsem.at[5]), pltpu.make_async_copy(dl_hbm, dl_ref, lsem.at[6]),
+             pltpu.make_async_copy(rates_hbm, rates_ref, lsem.at[7])]
+    for copy in small:
+        copy.start()
     own_h.start()
     own_o.start()
 
@@ -89,8 +95,6 @@
     peers += [(lax.rem(cp + d, 8), fs) for d in range(1, 8)]
     for peer in peers:
         pl.semaphore_signal(barrier, inc=1, device_id=peer, device_id_type=MESH)
-    pl.semaphore_wait(barrier, len(peers))
-
     def column(slot, core):
         dy, dz = SLOTS[slot]
         return ((lax.rem(zl + dz, 4) * 4 + lax.rem(y + dy, 4)) * 2 + core) * SHARD
@@ -119,22 +123,26 @@
         rows = pl.ds(0, 256) if part is None else pl.ds(part * 128, 128)
         return wobuf.at[0, slot, rows, pl.ds(h * 256, 256)]
 
-    def relay(view, sem, which, h, offset):
+    def relay(view, sem, which, h, offset, axes="yz"):
         for name, there, part in forwards(h, offset):
+            if name[0] not in axes:
+                continue
             pltpu.make_async_remote_copy(
                 src_ref=view(h, SLOT[offset], part), dst_ref=view(h, SLOT[there], part),
                 send_sem=send.at[which], recv_sem=sem.at[h, SLOT[there]],
                 device_id=link[name], device_id_type=MESH).start()
 
+    def opening(view, sem, which):
+        for h, axis in OPENING:
+            relay(view, sem, which, h, (0, 0), axis)
+
     def arrive(view, sem, h, offset):
         ref = view(h, SLOT[offset], None)
         pltpu.make_async_copy(ref, ref, sem.at[h, SLOT[offset]]).wait()
 
-    send_hidden(0)
-
-    for copy in own_w:
+    for copy in own_w + small:
         copy.wait()
-    gains = gain_ref[...]
+    gains = gain_ref[...].reshape(1, 512)
     gains = jnp.where(par == 0, gains[:, :256].astype(F32), gains[:, 256:].astype(F32))
     row = lax.broadcasted_iota(jnp.int32, (256, 256), 0)
     col = lax.broadcasted_iota(jnp.int32, (256, 256), 1)
@@ -142,8 +150,9 @@
     scaled = jnp.dot(diagonal, wraw[...], preferred_element_type=F32).astype(BF)
     wbuf[0, 0:128, :] = scaled[:128]
     wbuf[1, 0:128, :] = scaled[128:]
-    relay(w_view, wsem, 1, 0, (0, 0))
-    relay(w_view, wsem, 1, 1, (0, 0))
+    pl.semaphore_wait(barrier, len(peers))
+    send_hidden(0)
+    opening(w_view, wsem, 1)
     for pair in range(1, 8):
         send_hidden(pair)
 
@@ -195,8 +204,7 @@
         seen.add((h, o))
         if i == last:
             own_o.wait()
-            relay(o_view, osem, 2, 0, (0, 0))
-            relay(o_view, osem, 2, 1, (0, 0))
+            opening(o_view, osem, 2)
         while done < 8 and all((k, SLOTS[2 * done + e]) in seen for k in range(2) for e in range(2)):
             contract(done)
             done += 1
@@ -237,6 +245,8 @@
             value = value + prx[part, p].astype(F32)
         return value * scale
 
+    take_out(TAKE[0])
+    take_out(TAKE[1])
     kv = finish(1, slice(256, 512))
     kvbuf[512:640, 0:128] = rotate(kv[:, :128]).astype(BF)
     kvbuf[512:640, 128:256] = kv[:, 128:].astype(BF)
@@ -248,12 +258,12 @@
 
     for d in (1, 3, 2, 4):
         pl.when(cp + d < 8)(kv_copy(d).start)
-    take_out(2)
+    take_out(TAKE[2])
 
     qs = finish(0, slice(0, 256))
     qbuf[0:128, :] = (rotate(qs[:, :128]) * HD ** -0.5).astype(BF)
     qbuf[128:256, :] = (rotate(qs[:, 128:]) * HD ** -0.5).astype(BF)
-    take_out(2)
+    take_out(TAKE[3])
     for d in (2, 4, 1, 3):
         @pl.when(cp >= d)
         def _():
@@ -273,9 +283,7 @@
 
     def project(which, slot, core):
         o = jnp.dot(att[...], wobuf[which, slot], preferred_element_type=F32).astype(BF)
-        outv[which, slot] = o
-        at = pl.multiple_of(column(slot, core), SHARD)
-        pltpu.make_async_copy(outv.at[which, slot], out.at[:, pl.ds(at, SHARD)], outsem).start()
+        out[:, pl.ds(pl.multiple_of(column(slot, core), SHARD), SHARD)] = o
 
     def sibling_out(slot):
         ref = wobuf.at[1, slot]
@@ -312,22 +320,22 @@
     drain(prx, send.at[5])
     for d in (1, 2, 3, 4):
         pl.when(cp + d < 8)(kv_copy(d).wait_send)
-    drain(outv, outsem)
 
 
 def local(hidden, norm_gain, query_weight, key_weight, value_weight, out_weight, doc_lengths):
     rates = np.power(np.float32(THETA), -2.0 * np.arange(64, dtype=np.float32) / np.float32(128.0)).astype(np.float32)
     rates = jnp.asarray(np.concatenate([rates, rates])[None, :])
-    anywhere = pl.BlockSpec(memory_space=pl.ANY)
-    vmem = pl.BlockSpec(memory_space=pltpu.VMEM)
+    hbm = pl.BlockSpec(memory_space=pltpu.MemorySpace.HBM)
     dma = pltpu.SemaphoreType.DMA
     out = pl.pallas_call(
         kernel,
         out_shape=jax.ShapeDtypeStruct((ROWS, D), BF),
-        in_specs=[anywhere, vmem, anywhere, anywhere, anywhere, anywhere,
-                  pl.BlockSpec(memory_space=pltpu.SMEM), vmem],
-        out_specs=anywhere,
+        in_specs=[hbm] * 8,
+        out_specs=pl.BlockSpec(memory_space=pltpu.VMEM),
         scratch_shapes=[
+            pltpu.VMEM((512,), BF),
+            pltpu.SMEM((1, 4), jnp.int32),
+            pltpu.VMEM((1, 128), F32),
             pltpu.VMEM((ROWS, D), BF),
             pltpu.VMEM((256, 512), BF),
             pltpu.VMEM((2, NS * 128, 512), BF),
@@ -338,14 +346,13 @@
             pltpu.VMEM((2, 2, ROWS, 256), BF),
             pltpu.VMEM((5 * ROWS, 256), BF),
             pltpu.VMEM((2, NS, 256, 512), BF),
-            pltpu.VMEM((2, NS, ROWS, 512), BF),
             pltpu.VMEM((2 * ROWS, HD), BF),
             pltpu.VMEM((ROWS, 256), BF),
-            dma((5,)), dma((2, 8)), dma((2, NS)), dma((2, NS)), dma((NS,)), dma, dma((2, 2)), dma((4,)), dma,
+            dma((8,)), dma((2, 8)), dma((2, NS)), dma((2, NS)), dma((NS,)), dma, dma((2, 2)), dma((4,)),
             dma((6,)), dma((4,)),
         ],
         compiler_params=pltpu.CompilerParams(collective_id=0, has_side_effects=True, vmem_limit_bytes=48 << 20),
-    )(hidden[0], norm_gain[None, :], query_weight, key_weight, value_weight, out_weight, doc_lengths, rates)
+    )(*[pltpu.with_memory_space_constraint(a, pltpu.MemorySpace.HBM) for a in (hidden[0], norm_gain, query_weight, key_weight, value_weight, out_weight, doc_lengths, rates)])
     return out[None]
 
 

time: 82.8 us -> 69.6 us (0.84)
  Pallas kernels: 74.9 us -> 67.5 us
  local copies, waits for them, and re-layouts: 7.71 us -> 2.02 us
    pallas_call x1, Pallas kernels: 74.9 us -> 67.5 us  [local(): pl.pallas_call(kernel, out_shape=jax.ShapeDtypeStruct((ROWS, D), BF), in_...]
    unnamed x13 -> x1, local copies, waits for them, and re-layouts: 7.03 us -> 2.02 us
where the time goes in v2:
time: 69.6 us; the launch traced here: 69.5 us
  Pallas kernels  67.5 us (97%)
  local copies, waits for them, and re-layouts  2.02 us (3%)
    pallas_call x1, Pallas kernels, local(): pl.pallas_call(kernel, out_shape=jax.ShapeDtypeStruct((ROWS, D), BF), in_...  67.5 us
    unnamed x1, local copies, waits for them, and re-layouts  2.02 us

profile of v2, /device:TPU:1, one launch (start us, length us, event | category | flops | bytes accessed | tf_op | source)
XLA Modules:
  0.0 69.5 jit_solution(14940852233815560262)
XLA Ops:
  0.0 67.5 %shard_map.82 = bf16[128,16384]{1,0:T(8,128)(2,1)S(1)} custom-call(bf16[128,16384]{1,0:T(8,128)(2,1)} %bitcast.3, bf16[512]{0:T(512)(128)(2,1)} %gain_hbm.1, bf16[512,256]{1,0:T(8,128)(2,1)} %wq.1, bf16[512,128]{1,0:T(8,128)(2,1)} %wk.1, bf16[512,128]{1,0:T(8,128)(2,1)} %wv.1, bf16[256,512]{1,0:T(8,128)(2,1)} %wo.1, s32[1,4]{1,0:T(1,128)} %dl_hbm.1, ...), custom_call_target="tpu_custom_call" | custom-call | tf_op jit(solution)/shard_map/pallas_call | solution.py:330
  67.5 2.0 %copy.10 = bf16[1,128,16384]{2,1,0:T(8,128)(2,1)} copy(bf16[1,128,16384]{2,1,0:T(8,128)(2,1)S(1)} %bitcast.2) | data formatting | bytes 8388608

commit v3 on v2

--- a/solution.py
+++ b/solution.py
@@ -18,17 +18,26 @@
 BF = jnp.bfloat16
 F32 = jnp.float32
 
-SLOTS = [(0, 0), (1, 0), (3, 0), (0, 3), (3, 3), (1, 1), (1, 3), (0, 1), (3, 1), (2, 3), (2, 1), (1, 2), (3, 2), (0, 2),
-         (2, 0), (2, 2)]
+SLOTS = [
+    (0, 0), (0, 1), (0, 3), (1, 0), (3, 0), (1, 1), (3, 1), (3, 3), (1, 3), (0, 2), (2, 0), (2, 1), (3, 2), (2, 3),
+    (1, 2), (2, 2)
+]
 SLOT = {o: i for i, o in enumerate(SLOTS)}
 
-ORDER = [(0, (1, 0)), (1, (0, 3)), (0, (3, 0)), (1, (1, 0)), (1, (0, 1)), (1, (3, 3)), (1, (1, 3)), (1, (3, 0)),
-         (0, (2, 0)), (0, (1, 1)), (1, (0, 2)), (0, (0, 3)), (0, (3, 3)), (1, (1, 1)), (0, (3, 1)), (0, (1, 3)),
-         (0, (0, 1)), (0, (2, 3)), (0, (2, 1)), (1, (3, 1)), (1, (2, 3)), (1, (3, 2)), (1, (1, 2)), (1, (2, 1)),
-         (0, (1, 2)), (0, (3, 2)), (0, (0, 2)), (1, (2, 0)), (1, (2, 2)), (0, (2, 2))]
+PROGRAM = [
+    ("p", 0, "y"), ("w", 0, (3, 0)), ("w", 0, (1, 0)), ("w", 1, (0, 1)), ("w", 1, (0, 3)), ("w", 0, (0, 1)), ("w",
+    0, (0, 3)), ("w", 1, (1, 0)), ("w", 1, (3, 0)), ("w", 0, (2, 0)), ("w", 1, (0, 2)), ("w", 1, (3, 1)), ("w", 0,
+    (1, 1)), ("w", 1, (1, 1)), ("p", 1, "z"), ("w", 1, (1, 3)), ("w", 0, (2, 3)), ("w", 0, (3, 1)), ("w", 0, (3,
+    3)), ("w", 1, (3, 3)), ("w", 0, (2, 1)), ("w", 0, (1, 3)), ("w", 0, (0, 2)), ("w", 1, (3, 2)), ("w", 1, (1, 2)),
+    ("o", 1, (0, 3)), ("o", 1, (0, 1)), ("o", 0, (1, 0)), ("w", 1, (2, 0)), ("o", 0, (3, 0)), ("p", 1, "y"), ("w",
+    1, (2, 1)), ("w", 0, (3, 2)), ("w", 1, (2, 3)), ("w", 0, (1, 2)), ("w", 1, (2, 2)), ("w", 0, (2, 2)), ("c", 0),
+    ("p", 0, "z"), ("c", 1), ("c", 2), ("o", 1, (0, 2)), ("o", 0, (2, 0)), ("o", 0, (3, 3)), ("o", 1, (3, 3)), ("c",
+    3), ("o", 1, (1, 3)), ("o", 1, (3, 1)), ("o", 1, (3, 0)), ("o", 0, (1, 1)), ("o", 0, (0, 3)), ("o", 1, (1, 1)),
+    ("o", 0, (1, 3)), ("o", 0, (0, 1)), ("o", 1, (1, 2)), ("o", 0, (3, 1)), ("o", 1, (3, 2)), ("o", 1, (1, 0)),
+    ("o", 0, (2, 3)), ("o", 0, (2, 1)), ("c", 4), ("o", 1, (2, 3)), ("o", 0, (0, 2)), ("o", 0, (3, 2)), ("o", 1, (2,
+    1)), ("o", 1, (2, 0)), ("o", 0, (1, 2)), ("o", 1, (2, 2)), ("o", 0, (2, 2))
+]
 OPENING = ((0, "y"), (1, "z"), (0, "z"), (1, "y"))
-TAKE = (3, 2, 1, 6)
-
 
 def forwards(half, offset):
     p, q = offset if half == 0 else offset[::-1]
@@ -195,47 +204,32 @@
                 fresh = pair == 0 and (p == 0 or block >= 2)
                 acc[at] = piece if fresh else acc[at] + piece
 
-    seen = {(0, (0, 0)), (1, (0, 0))}
-    done = 0
-    last = max(i for i, (h, o) in enumerate(ORDER) if forwards(h, o))
-    for i, (h, o) in enumerate(ORDER):
-        arrive(w_view, wsem, h, o)
-        relay(w_view, wsem, 1, h, o)
-        seen.add((h, o))
-        if i == last:
-            own_o.wait()
-            opening(o_view, osem, 2)
-        while done < 8 and all((k, SLOTS[2 * done + e]) in seen for k in range(2) for e in range(2)):
-            contract(done)
-            done += 1
-
     def across(slot):
         return pltpu.make_async_remote_copy(
             src_ref=wobuf.at[0, slot], dst_ref=wobuf.at[1, slot], send_sem=send.at[3], recv_sem=dsem.at[slot],
             device_id=sibling, device_id_type=MESH)
 
-    o_seen = {(0, (0, 0)), (1, (0, 0))}
-
-    def take_out(count):
-        for h, o in ORDER[len(o_seen) - 2:len(o_seen) - 2 + count]:
-            arrive(o_view, osem, h, o)
-            relay(o_view, osem, 2, h, o)
-            o_seen.add((h, o))
-            if (1 - h, o) in o_seen:
-                across(SLOT[o]).start()
+    def project(which, slot, core):
+        o = jnp.dot(att[...], wobuf[which, slot], preferred_element_type=F32).astype(BF)
+        out[:, pl.ds(pl.multiple_of(column(slot, core), SHARD), SHARD)] = o
+
+    def sibling_out(slot):
+        ref = wobuf.at[1, slot]
+        pltpu.make_async_copy(ref, ref, dsem.at[slot]).wait()
+        project(1, slot, other)
 
     to_sibling = pltpu.make_async_remote_copy(
         src_ref=acc.at[pl.ds(3, 3)], dst_ref=srx, send_sem=send.at[4], recv_sem=ssem,
         device_id=sibling, device_id_type=MESH)
-    to_sibling.start()
-    across(0).start()
-    to_sibling.wait_recv()
-    for part, cols in ((1, slice(256, 512)), (0, slice(0, 256))):
-        for p in range(2):
-            ptx[part, p] = (acc[1 + p, :, cols] + srx[1 + p, :, cols]).astype(BF)
-            pltpu.make_async_remote_copy(
-                src_ref=ptx.at[part, p], dst_ref=prx.at[part, p], send_sem=send.at[5], recv_sem=psem.at[part, p],
-                device_id=device(partners[p], y, z, c), device_id_type=MESH).start()
+
+    def send_partials():
+        to_sibling.wait_recv()
+        for part, cols in ((1, slice(256, 512)), (0, slice(0, 256))):
+            for p in range(2):
+                ptx[part, p] = (acc[1 + p, :, cols] + srx[1 + p, :, cols]).astype(BF)
+                pltpu.make_async_remote_copy(
+                    src_ref=ptx.at[part, p], dst_ref=prx.at[part, p], send_sem=send.at[5], recv_sem=psem.at[part, p],
+                    device_id=device(partners[p], y, z, c), device_id_type=MESH).start()
 
     def finish(part, cols):
         value = acc[0, :, cols] + srx[0, :, cols]
@@ -245,69 +239,82 @@
             value = value + prx[part, p].astype(F32)
         return value * scale
 
-    take_out(TAKE[0])
-    take_out(TAKE[1])
-    kv = finish(1, slice(256, 512))
-    kvbuf[512:640, 0:128] = rotate(kv[:, :128]).astype(BF)
-    kvbuf[512:640, 128:256] = kv[:, 128:].astype(BF)
-
     def kv_copy(d):
         return pltpu.make_async_remote_copy(
-            src_ref=kvbuf.at[pl.ds(512, 128)], dst_ref=kvbuf.at[pl.ds((4 - d) * ROWS, ROWS)], send_sem=ksend.at[d - 1], recv_sem=ksem.at[d - 1],
+            src_ref=kvbuf.at[pl.ds(512, 128)], dst_ref=kvbuf.at[pl.ds((4 - d) * ROWS, ROWS)],
+            send_sem=ksend.at[d - 1], recv_sem=ksem.at[d - 1],
             device_id=(lax.rem(cp + d, 8), fs), device_id_type=MESH)
 
-    for d in (1, 3, 2, 4):
-        pl.when(cp + d < 8)(kv_copy(d).start)
-    take_out(TAKE[2])
-
-    qs = finish(0, slice(0, 256))
-    qbuf[0:128, :] = (rotate(qs[:, :128]) * HD ** -0.5).astype(BF)
-    qbuf[128:256, :] = (rotate(qs[:, 128:]) * HD ** -0.5).astype(BF)
-    take_out(TAKE[3])
-    for d in (2, 4, 1, 3):
-        @pl.when(cp >= d)
-        def _():
-            kv_copy(d).wait_recv()
-
-        @pl.when(cp < d)
-        def _():
-            kvbuf[(4 - d) * ROWS:(5 - d) * ROWS, :] = jnp.zeros((ROWS, 256), BF)
-
-    scores = lax.dot_general(qbuf[...], kvbuf[:, :128], (((1,), (1,)), ((), ())), preferred_element_type=F32)
-    keys = lax.broadcasted_iota(jnp.int32, (ROWS, 5 * ROWS), 1) + (cp - 4) * ROWS
-    allowed = (keys >= starts[:, :1]) & (keys <= places[:, :1])
-    e = jnp.where(jnp.concatenate([allowed, allowed], axis=0), jnp.exp(scores), 0.0)
-    mixed = jnp.dot(e.astype(BF), kvbuf[:, 128:], preferred_element_type=F32) / jnp.sum(e, axis=1, keepdims=True)
-    att[:, 0:128] = mixed[:128].astype(BF)
-    att[:, 128:256] = mixed[128:].astype(BF)
-
-    def project(which, slot, core):
-        o = jnp.dot(att[...], wobuf[which, slot], preferred_element_type=F32).astype(BF)
-        out[:, pl.ds(pl.multiple_of(column(slot, core), SHARD), SHARD)] = o
-
-    def sibling_out(slot):
-        ref = wobuf.at[1, slot]
-        pltpu.make_async_copy(ref, ref, dsem.at[slot]).wait()
-        project(1, slot, other)
-
-    ready = [s for s in range(NS) if (0, SLOTS[s]) in o_seen and (1, SLOTS[s]) in o_seen]
-    projected = set()
-    pending = []
-    for s in ready:
-        project(0, s, c)
-        projected.add(s)
-        pending.append(s)
-    while len(o_seen) < 32:
-        take_out(1)
-        for s in range(NS):
-            if s not in projected and (0, SLOTS[s]) in o_seen and (1, SLOTS[s]) in o_seen:
-                project(0, s, c)
-                projected.add(s)
-                pending.append(s)
-        if len(pending) > 2:
-            sibling_out(pending.pop(0))
-    for s in pending:
-        sibling_out(s)
+    def share_kv():
+        kv = finish(1, slice(256, 512))
+        kvbuf[512:640, 0:128] = rotate(kv[:, :128]).astype(BF)
+        kvbuf[512:640, 128:256] = kv[:, 128:].astype(BF)
+        for d in (1, 3, 2, 4):
+            pl.when(cp + d < 8)(kv_copy(d).start)
+
+    def make_queries():
+        qs = finish(0, slice(0, 256))
+        qbuf[0:128, :] = (rotate(qs[:, :128]) * HD ** -0.5).astype(BF)
+        qbuf[128:256, :] = (rotate(qs[:, 128:]) * HD ** -0.5).astype(BF)
+
+    def attend():
+        for d in (2, 4, 1, 3):
+            @pl.when(cp >= d)
+            def _():
+                kv_copy(d).wait_recv()
+
+            @pl.when(cp < d)
+            def _():
+                kvbuf[(4 - d) * ROWS:(5 - d) * ROWS, :] = jnp.zeros((ROWS, 256), BF)
+
+        scores = lax.dot_general(qbuf[...], kvbuf[:, :128], (((1,), (1,)), ((), ())), preferred_element_type=F32)
+        keys = lax.broadcasted_iota(jnp.int32, (ROWS, 5 * ROWS), 1) + (cp - 4) * ROWS
+        allowed = (keys >= starts[:, :1]) & (keys <= places[:, :1])
+        e = jnp.where(jnp.concatenate([allowed, allowed], axis=0), jnp.exp(scores), 0.0)
+        mixed = jnp.dot(e.astype(BF), kvbuf[:, 128:], preferred_element_type=F32) / jnp.sum(e, axis=1, keepdims=True)
+        att[:, 0:128] = mixed[:128].astype(BF)
+        att[:, 128:256] = mixed[128:].astype(BF)
+
+    chain = [to_sibling.start, send_partials, share_kv, make_queries, attend]
+    seen = {("w", 0, (0, 0)), ("w", 1, (0, 0)), ("o", 0, (0, 0)), ("o", 1, (0, 0))}
+    contracted, attended, ready, pending = 0, False, [], []
+
+    def out_ready(slot):
+        across(slot).start()
+        (pending if attended else ready).append(slot)
+        if attended:
+            project(0, slot, c)
+
+    for step in PROGRAM:
+        if step[0] == "c":
+            chain[step[1]]()
+            if step[1] == 4:
+                attended = True
+                for slot in ready:
+                    project(0, slot, c)
+                pending += ready
+        elif step[0] == "p":
+            if ("started",) not in seen:
+                seen.add(("started",))
+                own_o.wait()
+                out_ready(0)
+            relay(o_view, osem, 2, step[1], (0, 0), step[2])
+        else:
+            kind, h, o = step
+            view, sem, which = (w_view, wsem, 1) if kind == "w" else (o_view, osem, 2)
+            arrive(view, sem, h, o)
+            relay(view, sem, which, h, o)
+            seen.add(step)
+            if kind == "o" and (kind, 1 - h, o) in seen:
+                out_ready(SLOT[o])
+            while contracted < 8 and all(("w", k, SLOTS[2 * contracted + e]) in seen for k in range(2) for e in range(2)):
+                contract(contracted)
+                contracted += 1
+        if attended:
+            while len(pending) > 2:
+                sibling_out(pending.pop(0))
+    for slot in pending:
+        sibling_out(slot)
 
     def drain(ref, sem):
         pltpu.make_async_copy(ref, ref, sem).wait()

time: 69.6 us -> 65.4 us (0.940)
  Pallas kernels: 67.5 us -> 63.3 us
    pallas_call x1, Pallas kernels: 67.5 us -> 63.3 us  [local(): pl.pallas_call(kernel, out_shape=jax.ShapeDtypeStruct((ROWS, D), BF), in_...]
where the time goes in v3:
time: 65.4 us; the launch traced here: 65.3 us
  Pallas kernels  63.3 us (97%)
  local copies, waits for them, and re-layouts  2.02 us (3%)
    pallas_call x1, Pallas kernels, local(): pl.pallas_call(kernel, out_shape=jax.ShapeDtypeStruct((ROWS, D), BF), in_...  63.3 us
    unnamed x1, local copies, waits for them, and re-layouts  2.02 us

profile of v3, /device:TPU:1, one launch (start us, length us, event | category | flops | bytes accessed | tf_op | source)
XLA Modules:
  0.0 65.3 jit_solution(11772963456870014938)
XLA Ops:
  0.0 63.3 %shard_map.82 = bf16[128,16384]{1,0:T(8,128)(2,1)S(1)} custom-call(bf16[128,16384]{1,0:T(8,128)(2,1)} %bitcast.3, bf16[512]{0:T(512)(128)(2,1)} %gain_hbm.1, bf16[512,256]{1,0:T(8,128)(2,1)} %wq.1, bf16[512,128]{1,0:T(8,128)(2,1)} %wk.1, bf16[512,128]{1,0:T(8,128)(2,1)} %wv.1, bf16[256,512]{1,0:T(8,128)(2,1)} %wo.1, s32[1,4]{1,0:T(1,128)} %dl_hbm.1, ...), custom_call_target="tpu_custom_call" | custom-call | tf_op jit(solution)/shard_map/pallas_call | solution.py:337
  63.3 2.0 %copy.10 = bf16[1,128,16384]{2,1,0:T(8,128)(2,1)} copy(bf16[1,128,16384]{2,1,0:T(8,128)(2,1)S(1)} %bitcast.2) | data formatting | bytes 8388608

commit v4 on v3

--- a/solution.py
+++ b/solution.py
@@ -15,27 +15,29 @@
 SHARD = 512
 HD = 128
 NS = 16
+W_CUT = 64
+O_CUT = 112
 BF = jnp.bfloat16
 F32 = jnp.float32
 
 SLOTS = [
-    (0, 0), (0, 1), (0, 3), (1, 0), (3, 0), (1, 1), (3, 1), (3, 3), (1, 3), (0, 2), (2, 0), (2, 1), (3, 2), (2, 3),
-    (1, 2), (2, 2)
+    (0, 0), (0, 1), (1, 1), (3, 0), (3, 1), (3, 3), (1, 0), (0, 3), (1, 3), (1, 2), (2, 1), (2, 0), (0, 2), (3, 2),
+    (2, 3), (2, 2)
 ]
 SLOT = {o: i for i, o in enumerate(SLOTS)}
 
 PROGRAM = [
-    ("p", 0, "y"), ("w", 0, (3, 0)), ("w", 0, (1, 0)), ("w", 1, (0, 1)), ("w", 1, (0, 3)), ("w", 0, (0, 1)), ("w",
-    0, (0, 3)), ("w", 1, (1, 0)), ("w", 1, (3, 0)), ("w", 0, (2, 0)), ("w", 1, (0, 2)), ("w", 1, (3, 1)), ("w", 0,
-    (1, 1)), ("w", 1, (1, 1)), ("p", 1, "z"), ("w", 1, (1, 3)), ("w", 0, (2, 3)), ("w", 0, (3, 1)), ("w", 0, (3,
-    3)), ("w", 1, (3, 3)), ("w", 0, (2, 1)), ("w", 0, (1, 3)), ("w", 0, (0, 2)), ("w", 1, (3, 2)), ("w", 1, (1, 2)),
-    ("o", 1, (0, 3)), ("o", 1, (0, 1)), ("o", 0, (1, 0)), ("w", 1, (2, 0)), ("o", 0, (3, 0)), ("p", 1, "y"), ("w",
-    1, (2, 1)), ("w", 0, (3, 2)), ("w", 1, (2, 3)), ("w", 0, (1, 2)), ("w", 1, (2, 2)), ("w", 0, (2, 2)), ("c", 0),
-    ("p", 0, "z"), ("c", 1), ("c", 2), ("o", 1, (0, 2)), ("o", 0, (2, 0)), ("o", 0, (3, 3)), ("o", 1, (3, 3)), ("c",
-    3), ("o", 1, (1, 3)), ("o", 1, (3, 1)), ("o", 1, (3, 0)), ("o", 0, (1, 1)), ("o", 0, (0, 3)), ("o", 1, (1, 1)),
-    ("o", 0, (1, 3)), ("o", 0, (0, 1)), ("o", 1, (1, 2)), ("o", 0, (3, 1)), ("o", 1, (3, 2)), ("o", 1, (1, 0)),
-    ("o", 0, (2, 3)), ("o", 0, (2, 1)), ("c", 4), ("o", 1, (2, 3)), ("o", 0, (0, 2)), ("o", 0, (3, 2)), ("o", 1, (2,
-    1)), ("o", 1, (2, 0)), ("o", 0, (1, 2)), ("o", 1, (2, 2)), ("o", 0, (2, 2))
+    ("w", 0, (3, 0)), ("w", 0, (1, 0)), ("w", 1, (0, 1)), ("p", 0, "y"), ("w", 1, (0, 3)), ("w", 0, (2, 0)), ("w",
+    0, (0, 1)), ("w", 0, (1, 1)), ("w", 0, (1, 3)), ("w", 1, (1, 1)), ("w", 1, (3, 0)), ("w", 0, (3, 3)), ("w", 1,
+    (0, 2)), ("p", 1, "z"), ("w", 0, (3, 1)), ("w", 1, (3, 1)), ("w", 1, (3, 3)), ("w", 1, (1, 0)), ("w", 0, (0,
+    3)), ("w", 1, (1, 3)), ("w", 0, (2, 3)), ("w", 0, (1, 2)), ("w", 0, (2, 1)), ("w", 1, (3, 2)), ("w", 1, (1, 2)),
+    ("o", 0, (1, 0)), ("o", 0, (3, 0)), ("p", 1, "y"), ("w", 1, (2, 1)), ("o", 1, (0, 3)), ("w", 1, (2, 0)), ("o",
+    1, (0, 1)), ("w", 0, (0, 2)), ("w", 0, (3, 2)), ("w", 0, (2, 2)), ("w", 1, (2, 3)), ("w", 1, (2, 2)), ("c", 0),
+    ("c", 1), ("o", 0, (2, 0)), ("p", 0, "z"), ("o", 1, (0, 2)), ("o", 1, (3, 3)), ("c", 2), ("o", 0, (3, 3)), ("o",
+    0, (3, 1)), ("o", 1, (3, 0)), ("o", 0, (1, 1)), ("o", 1, (1, 3)), ("o", 0, (2, 3)), ("c", 3), ("o", 0, (1, 3)),
+    ("o", 1, (1, 1)), ("o", 0, (2, 1)), ("o", 0, (0, 1)), ("o", 1, (1, 0)), ("o", 1, (3, 2)), ("o", 0, (0, 3)),
+    ("o", 1, (1, 2)), ("o", 1, (3, 1)), ("c", 4), ("o", 1, (2, 0)), ("o", 1, (2, 3)), ("o", 1, (2, 2)), ("o", 0, (2,
+    2)), ("o", 1, (2, 1)), ("o", 0, (1, 2)), ("o", 0, (3, 2)), ("o", 0, (0, 2))
 ]
 OPENING = ((0, "y"), (1, "z"), (0, "z"), (1, "y"))
 
@@ -125,12 +127,12 @@
         pltpu.make_async_copy(ref, ref, hsem.at[p, pair]).wait()
 
     def w_view(h, slot, part):
-        rows, cols = pl.ds(slot * 128, 128), pl.ds(h * 256, 256)
-        return wbuf.at[:, rows, cols] if part is None else wbuf.at[part, rows, cols]
+        rows = pl.ds(slot * 128 + (0, W_CUT)[h], (W_CUT, 128 - W_CUT)[h])
+        return wbuf.at[:, rows] if part is None else wbuf.at[part, rows]
 
     def o_view(h, slot, part):
-        rows = pl.ds(0, 256) if part is None else pl.ds(part * 128, 128)
-        return wobuf.at[0, slot, rows, pl.ds(h * 256, 256)]
+        rows = pl.ds((0, O_CUT)[h], (O_CUT, 256 - O_CUT)[h])
+        return wobuf.at[0, slot, rows] if part is None else wobuf.at[0, slot, rows, pl.ds(part * 256, 256)]
 
     def relay(view, sem, which, h, offset, axes="yz"):
         for name, there, part in forwards(h, offset):

time: 65.4 us -> 64.3 us (0.983)
  Pallas kernels: 63.3 us -> 62.2 us
    pallas_call x1, Pallas kernels: 63.3 us -> 62.2 us  [local(): pl.pallas_call(kernel, out_shape=jax.ShapeDtypeStruct((ROWS, D), BF), in_...]
where the time goes in v4:
time: 64.3 us; the launch traced here: 64.2 us
  Pallas kernels  62.2 us (97%)
  local copies, waits for them, and re-layouts  2.02 us (3%)
    pallas_call x1, Pallas kernels, local(): pl.pallas_call(kernel, out_shape=jax.ShapeDtypeStruct((ROWS, D), BF), in_...  62.2 us
    unnamed x1, local copies, waits for them, and re-layouts  2.02 us

profile of v4, /device:TPU:1, one launch (start us, length us, event | category | flops | bytes accessed | tf_op | source)
XLA Modules:
  0.0 64.2 jit_solution(15990774794581667430)
XLA Ops:
  0.0 62.2 %shard_map.82 = bf16[128,16384]{1,0:T(8,128)(2,1)S(1)} custom-call(bf16[128,16384]{1,0:T(8,128)(2,1)} %bitcast.3, bf16[512]{0:T(512)(128)(2,1)} %gain_hbm.1, bf16[512,256]{1,0:T(8,128)(2,1)} %wq.1, bf16[512,128]{1,0:T(8,128)(2,1)} %wk.1, bf16[512,128]{1,0:T(8,128)(2,1)} %wv.1, bf16[256,512]{1,0:T(8,128)(2,1)} %wo.1, s32[1,4]{1,0:T(1,128)} %dl_hbm.1, ...), custom_call_target="tpu_custom_call" | custom-call | tf_op jit(solution)/shard_map/pallas_call | solution.py:339
  62.2 2.0 %copy.10 = bf16[1,128,16384]{2,1,0:T(8,128)(2,1)} copy(bf16[1,128,16384]{2,1,0:T(8,128)(2,1)S(1)} %bitcast.2) | data formatting | bytes 8388608

commit v5 on v4

--- a/solution.py
+++ b/solution.py
@@ -21,23 +21,26 @@
 F32 = jnp.float32
 
 SLOTS = [
-    (0, 0), (0, 1), (1, 1), (3, 0), (3, 1), (3, 3), (1, 0), (0, 3), (1, 3), (1, 2), (2, 1), (2, 0), (0, 2), (3, 2),
-    (2, 3), (2, 2)
+    (0, 0), (0, 1), (0, 3), (1, 0), (3, 1), (3, 0), (1, 1), (3, 3), (1, 3), (0, 2), (2, 0), (2, 3), (1, 2), (2, 1),
+    (3, 2), (2, 2)
 ]
 SLOT = {o: i for i, o in enumerate(SLOTS)}
 
 PROGRAM = [
-    ("w", 0, (3, 0)), ("w", 0, (1, 0)), ("w", 1, (0, 1)), ("p", 0, "y"), ("w", 1, (0, 3)), ("w", 0, (2, 0)), ("w",
-    0, (0, 1)), ("w", 0, (1, 1)), ("w", 0, (1, 3)), ("w", 1, (1, 1)), ("w", 1, (3, 0)), ("w", 0, (3, 3)), ("w", 1,
-    (0, 2)), ("p", 1, "z"), ("w", 0, (3, 1)), ("w", 1, (3, 1)), ("w", 1, (3, 3)), ("w", 1, (1, 0)), ("w", 0, (0,
-    3)), ("w", 1, (1, 3)), ("w", 0, (2, 3)), ("w", 0, (1, 2)), ("w", 0, (2, 1)), ("w", 1, (3, 2)), ("w", 1, (1, 2)),
-    ("o", 0, (1, 0)), ("o", 0, (3, 0)), ("p", 1, "y"), ("w", 1, (2, 1)), ("o", 1, (0, 3)), ("w", 1, (2, 0)), ("o",
-    1, (0, 1)), ("w", 0, (0, 2)), ("w", 0, (3, 2)), ("w", 0, (2, 2)), ("w", 1, (2, 3)), ("w", 1, (2, 2)), ("c", 0),
-    ("c", 1), ("o", 0, (2, 0)), ("p", 0, "z"), ("o", 1, (0, 2)), ("o", 1, (3, 3)), ("c", 2), ("o", 0, (3, 3)), ("o",
-    0, (3, 1)), ("o", 1, (3, 0)), ("o", 0, (1, 1)), ("o", 1, (1, 3)), ("o", 0, (2, 3)), ("c", 3), ("o", 0, (1, 3)),
-    ("o", 1, (1, 1)), ("o", 0, (2, 1)), ("o", 0, (0, 1)), ("o", 1, (1, 0)), ("o", 1, (3, 2)), ("o", 0, (0, 3)),
-    ("o", 1, (1, 2)), ("o", 1, (3, 1)), ("c", 4), ("o", 1, (2, 0)), ("o", 1, (2, 3)), ("o", 1, (2, 2)), ("o", 0, (2,
-    2)), ("o", 1, (2, 1)), ("o", 0, (1, 2)), ("o", 0, (3, 2)), ("o", 0, (0, 2))
+    ("p", 1, "z"), ("w", 0, (1, 0)), ("w", 1, (0, 3)), ("w", 1, (0, 1)), ("w", 0, (3, 0)), ("w", 0, (0, 1)), ("p",
+    0, "y"), ("o", 1, (0, 1)), ("w", 0, (1, 3)), ("w", 1, (0, 2)), ("w", 1, (1, 1)), ("w", 1, (3, 1)), ("w", 0, (2,
+    0)), ("w", 0, (0, 3)), ("w", 1, (3, 3)), ("o", 0, (1, 0)), ("w", 1, (1, 0)), ("w", 0, (3, 1)), ("w", 1, (3, 0)),
+    ("w", 0, (1, 1)), ("w", 0, (3, 3)), ("w", 1, (1, 3)), ("w", 0, (2, 1)), ("w", 1, (3, 2)), ("w", 0, (2, 3)),
+    ("o", 1, (3, 1)), ("w", 1, (1, 2)), ("w", 0, (0, 2)), ("o", 0, (1, 1)), ("o", 0, (3, 0)), ("o", 1, (1, 1)),
+    ("w", 1, (2, 0)), ("o", 0, (1, 3)), ("o", 1, (0, 3)), ("w", 1, (2, 3)), ("w", 0, (1, 2)), ("w", 1, (2, 1)),
+    ("p", 0, "z"), ("w", 0, (3, 2)), ("w", 0, (2, 2)), ("w", 1, (2, 2)), ("c", 0), ("x", 1, (0, 1)), ("x", 0, (1,
+    0)), ("o", 0, (3, 1)), ("p", 1, "y"), ("c", 1), ("o", 0, (0, 1)), ("x", 0, (1, 1)), ("x", 1, (1, 1)), ("o", 0,
+    (2, 0)), ("o", 1, (1, 3)), ("o", 1, (0, 2)), ("c", 2), ("x", 1, (3, 1)), ("o", 1, (1, 0)), ("x", 1, (1, 3)),
+    ("o", 0, (3, 3)), ("x", 0, (3, 1)), ("o", 0, (1, 2)), ("x", 0, (1, 3)), ("o", 1, (3, 0)), ("x", 0, (3, 0)),
+    ("o", 1, (3, 3)), ("o", 0, (0, 3)), ("o", 1, (3, 2)), ("o", 0, (2, 3)), ("x", 0, (0, 1)), ("o", 1, (1, 2)),
+    ("x", 1, (1, 0)), ("o", 0, (2, 1)), ("c", 3), ("c", 4), ("o", 1, (2, 3)), ("o", 0, (0, 2)), ("x", 1, (0, 3)),
+    ("o", 1, (2, 1)), ("o", 0, (3, 2)), ("o", 1, (2, 2)), ("o", 1, (2, 0)), ("x", 1, (3, 0)), ("x", 0, (0, 3)),
+    ("o", 0, (2, 2)), ("x", 1, (3, 3)), ("x", 0, (3, 3))
 ]
 OPENING = ((0, "y"), (1, "z"), (0, "z"), (1, "y"))
 
@@ -61,14 +64,18 @@
     return out
 
 
+def last(offset):
+    return 2 in offset
+
+
 def device(x, y, z, c):
     x, y, z = lax.rem(x + 4, 4), lax.rem(y + 4, 4), lax.rem(z + 8, 8)
     return (x * 2 + z // 4, ((lax.rem(z, 4) * 4) + y) * 2 + c)
 
 
 def kernel(hid, gain_hbm, wq, wk, wv, wo, dl_hbm, rates_hbm, out,
-           gain_ref, dl_ref, rates_ref, hown, wraw, wbuf, xbuf, acc, srx, ptx, prx, kvbuf, wobuf, qbuf, att,
-           lsem, hsem, wsem, osem, dsem, ssem, psem, ksem, send, ksend):
+           gain_ref, dl_ref, rates_ref, hown, wraw, wbuf, xbuf, acc, srx, ptx, prx, kvbuf, wobuf, qbuf, att, stage,
+           lsem, hsem, wsem, osem, dsem, asem, ssem, psem, ksem, xsem, send, ksend):
     cp, fs = lax.axis_index("cp"), lax.axis_index("fsdp")
     x, zh = cp // 2, lax.rem(cp, 2)
     c = lax.rem(fs, 2)
@@ -130,9 +137,45 @@
         rows = pl.ds(slot * 128 + (0, W_CUT)[h], (W_CUT, 128 - W_CUT)[h])
         return wbuf.at[:, rows] if part is None else wbuf.at[part, rows]
 
-    def o_view(h, slot, part):
+    def o_view(h, slot, part=None):
         rows = pl.ds((0, O_CUT)[h], (O_CUT, 256 - O_CUT)[h])
-        return wobuf.at[0, slot, rows] if part is None else wobuf.at[0, slot, rows, pl.ds(part * 256, 256)]
+        if part is None:
+            return wobuf.at[0, slot, rows]
+        return wobuf.at[0, slot, rows, pl.ds(pl.multiple_of(part * 256, 256), 256)]
+
+    def o_send(name, h, offset, there, part):
+        pltpu.make_async_remote_copy(
+            src_ref=o_view(h, SLOT[offset], part), dst_ref=o_view(h, SLOT[there], part),
+            send_sem=send.at[2], recv_sem=osem.at[h, SLOT[there]], device_id=link[name], device_id_type=MESH).start()
+
+    def relay_out(h, offset, axes="yz"):
+        for name, there, part in forwards(h, offset):
+            if name[0] not in axes:
+                continue
+            if not last(there):
+                o_send(name, h, offset, there, par)
+            elif part is None:
+                o_send(name, h, offset, there, None)
+            elif last(offset) or part == 0:
+                o_send(name, h, offset, there, par if part == 0 else 1 - par)
+        if offset != (0, 0) and not last(offset):
+            swap = o_view(h, SLOT[offset], par)
+            pltpu.make_async_remote_copy(
+                src_ref=swap, dst_ref=swap, send_sem=send.at[6], recv_sem=xsem.at[h, SLOT[offset]],
+                device_id=device(partners[h], y, z, c), device_id_type=MESH).start()
+
+    def relay_rest(h, offset):
+        for name, there, part in forwards(h, offset):
+            if last(there) and part == 1:
+                o_send(name, h, offset, there, 1 - par)
+
+    def arrive_out(h, offset):
+        ref = o_view(h, SLOT[offset], None if last(offset) else 0)
+        pltpu.make_async_copy(ref, ref, osem.at[h, SLOT[offset]]).wait()
+
+    def arrive_rest(h, offset):
+        ref = o_view(h, SLOT[offset], 0)
+        pltpu.make_async_copy(ref, ref, xsem.at[h, SLOT[offset]]).wait()
 
     def relay(view, sem, which, h, offset, axes="yz"):
         for name, there, part in forwards(h, offset):
@@ -206,19 +249,17 @@
                 fresh = pair == 0 and (p == 0 or block >= 2)
                 acc[at] = piece if fresh else acc[at] + piece
 
-    def across(slot):
-        return pltpu.make_async_remote_copy(
-            src_ref=wobuf.at[0, slot], dst_ref=wobuf.at[1, slot], send_sem=send.at[3], recv_sem=dsem.at[slot],
-            device_id=sibling, device_id_type=MESH)
-
-    def project(which, slot, core):
-        o = jnp.dot(att[...], wobuf[which, slot], preferred_element_type=F32).astype(BF)
-        out[:, pl.ds(pl.multiple_of(column(slot, core), SHARD), SHARD)] = o
-
-    def sibling_out(slot):
-        ref = wobuf.at[1, slot]
-        pltpu.make_async_copy(ref, ref, dsem.at[slot]).wait()
-        project(1, slot, other)
+    swap_attended = pltpu.make_async_remote_copy(
+        src_ref=att.at[0], dst_ref=att.at[1], send_sem=send.at[7], recv_sem=asem, device_id=sibling, device_id_type=MESH)
+
+    def project(slot):
+        o = jnp.dot(att[...].reshape(256, 256), wobuf[0, slot], preferred_element_type=F32).astype(BF)
+        cols = pl.ds(pl.multiple_of(column(slot, c), SHARD), SHARD)
+        out[:, cols] = o[:128]
+        stage[slot] = o[128:]
+        pltpu.make_async_remote_copy(
+            src_ref=stage.at[slot], dst_ref=out.at[:, cols], send_sem=send.at[3], recv_sem=dsem,
+            device_id=sibling, device_id_type=MESH).start()
 
     to_sibling = pltpu.make_async_remote_copy(
         src_ref=acc.at[pl.ds(3, 3)], dst_ref=srx, send_sem=send.at[4], recv_sem=ssem,
@@ -274,18 +315,20 @@
         allowed = (keys >= starts[:, :1]) & (keys <= places[:, :1])
         e = jnp.where(jnp.concatenate([allowed, allowed], axis=0), jnp.exp(scores), 0.0)
         mixed = jnp.dot(e.astype(BF), kvbuf[:, 128:], preferred_element_type=F32) / jnp.sum(e, axis=1, keepdims=True)
-        att[:, 0:128] = mixed[:128].astype(BF)
-        att[:, 128:256] = mixed[128:].astype(BF)
+        att[0, :, 0:128] = mixed[:128].astype(BF)
+        att[0, :, 128:256] = mixed[128:].astype(BF)
+        swap_attended.start()
+        swap_attended.wait_recv()
 
     chain = [to_sibling.start, send_partials, share_kv, make_queries, attend]
     seen = {("w", 0, (0, 0)), ("w", 1, (0, 0)), ("o", 0, (0, 0)), ("o", 1, (0, 0))}
-    contracted, attended, ready, pending = 0, False, [], []
+    contracted, attended, ready = 0, False, []
 
     def out_ready(slot):
-        across(slot).start()
-        (pending if attended else ready).append(slot)
         if attended:
-            project(0, slot, c)
+            project(slot)
+        else:
+            ready.append(slot)
 
     for step in PROGRAM:
         if step[0] == "c":
@@ -293,38 +336,41 @@
             if step[1] == 4:
                 attended = True
                 for slot in ready:
-                    project(0, slot, c)
-                pending += ready
+                    project(slot)
         elif step[0] == "p":
             if ("started",) not in seen:
                 seen.add(("started",))
                 own_o.wait()
                 out_ready(0)
-            relay(o_view, osem, 2, step[1], (0, 0), step[2])
+            relay_out(step[1], (0, 0), step[2])
         else:
             kind, h, o = step
-            view, sem, which = (w_view, wsem, 1) if kind == "w" else (o_view, osem, 2)
-            arrive(view, sem, h, o)
-            relay(view, sem, which, h, o)
+            if kind == "w":
+                arrive(w_view, wsem, h, o)
+                relay(w_view, wsem, 1, h, o)
+            elif kind == "o":
+                arrive_out(h, o)
+                relay_out(h, o)
+            else:
+                arrive_rest(h, o)
+                relay_rest(h, o)
             seen.add(step)
-            if kind == "o" and (kind, 1 - h, o) in seen:
+            if kind == ("o" if last(o) else "x") and (kind, 1 - h, o) in seen:
                 out_ready(SLOT[o])
             while contracted < 8 and all(("w", k, SLOTS[2 * contracted + e]) in seen for k in range(2) for e in range(2)):
                 contract(contracted)
                 contracted += 1
-        if attended:
-            while len(pending) > 2:
-                sibling_out(pending.pop(0))
-    for slot in pending:
-        sibling_out(slot)
 
     def drain(ref, sem):
         pltpu.make_async_copy(ref, ref, sem).wait()
 
     drain(xbuf, send.at[0])
     drain(wbuf.at[:, pl.ds(128, 15 * 128)], send.at[1])
-    drain(wobuf.at[0, pl.ds(1, 15)], send.at[2])
-    drain(wobuf.at[1], send.at[3])
+    drain(wobuf.at[0, pl.ds(0, 11)], send.at[2])
+    drain(wobuf.at[0, pl.ds(0, 4)], send.at[6])
+    drain(stage, send.at[3])
+    drain(stage, dsem)
+    swap_attended.wait_send()
     drain(srx, send.at[4])
     drain(prx, send.at[5])
     for d in (1, 2, 3, 4):
@@ -354,11 +400,12 @@
             pltpu.VMEM((2, 2, ROWS, 256), BF),
             pltpu.VMEM((2, 2, ROWS, 256), BF),
             pltpu.VMEM((5 * ROWS, 256), BF),
-            pltpu.VMEM((2, NS, 256, 512), BF),
+            pltpu.VMEM((1, NS, 256, 512), BF),
             pltpu.VMEM((2 * ROWS, HD), BF),
-            pltpu.VMEM((ROWS, 256), BF),
-            dma((8,)), dma((2, 8)), dma((2, NS)), dma((2, NS)), dma((NS,)), dma, dma((2, 2)), dma((4,)),
-            dma((6,)), dma((4,)),
+            pltpu.VMEM((2, ROWS, 256), BF),
+            pltpu.VMEM((NS, ROWS, 512), BF),
+            dma((8,)), dma((2, 8)), dma((2, NS)), dma((2, NS)), dma, dma, dma, dma((2, 2)), dma((4,)),
+            dma((2, NS)), dma((8,)), dma((4,)),
         ],
         compiler_params=pltpu.CompilerParams(collective_id=0, has_side_effects=True, vmem_limit_bytes=48 << 20),
     )(*[pltpu.with_memory_space_constraint(a, pltpu.MemorySpace.HBM) for a in (hidden[0], norm_gain, query_weight, key_weight, value_weight, out_weight, doc_lengths, rates)])

time: 64.3 us -> 63 us (0.980)
  Pallas kernels: 62.2 us -> 60.4 us
    pallas_call x1, Pallas kernels: 62.2 us -> 60.4 us  [local(): pl.pallas_call(kernel, out_shape=jax.ShapeDtypeStruct((ROWS, D), BF), in_...]
where the time goes in v5:
time: 63 us; the launch traced here: 62.5 us
  Pallas kernels  60.4 us (96%)
  local copies, waits for them, and re-layouts  2.02 us (3%)
    pallas_call x1, Pallas kernels, local(): pl.pallas_call(kernel, out_shape=jax.ShapeDtypeStruct((ROWS, D), BF), in_...  60.4 us
    unnamed x1, local copies, waits for them, and re-layouts  2.02 us

profile of v5, /device:TPU:1, one launch (start us, length us, event | category | flops | bytes accessed | tf_op | source)
XLA Modules:
  0.0 62.5 jit_solution(15769662897751192116)
XLA Ops:
  0.0 60.4 %shard_map.82 = bf16[128,16384]{1,0:T(8,128)(2,1)S(1)} custom-call(bf16[128,16384]{1,0:T(8,128)(2,1)} %bitcast.3, bf16[512]{0:T(512)(128)(2,1)} %gain_hbm.1, bf16[512,256]{1,0:T(8,128)(2,1)} %wq.1, bf16[512,128]{1,0:T(8,128)(2,1)} %wk.1, bf16[512,128]{1,0:T(8,128)(2,1)} %wv.1, bf16[256,512]{1,0:T(8,128)(2,1)} %wo.1, s32[1,4]{1,0:T(1,128)} %dl_hbm.1, ...), custom_call_target="tpu_custom_call" | custom-call | tf_op jit(solution)/shard_map/pallas_call | solution.py:385
  60.4 2.0 %copy.10 = bf16[1,128,16384]{2,1,0:T(8,128)(2,1)} copy(bf16[1,128,16384]{2,1,0:T(8,128)(2,1)S(1)} %bitcast.2) | data formatting | bytes 8388608

commit v6 on v5

--- a/solution.py
+++ b/solution.py
@@ -205,9 +205,8 @@
     wbuf[0, 0:128, :] = scaled[:128]
     wbuf[1, 0:128, :] = scaled[128:]
     pl.semaphore_wait(barrier, len(peers))
-    send_hidden(0)
     opening(w_view, wsem, 1)
-    for pair in range(1, 8):
+    for pair in range(8):
         send_hidden(pair)
 
     own_h.wait()

time: 63 us -> 63 us (level)
  no operation moved by 1% of the time
where the time goes in v6:
time: 63 us; the launch traced here: 62.4 us
  Pallas kernels  60.4 us (96%)
  local copies, waits for them, and re-layouts  2.02 us (3%)
    pallas_call x1, Pallas kernels, local(): pl.pallas_call(kernel, out_shape=jax.ShapeDtypeStruct((ROWS, D), BF), in_...  60.4 us
    unnamed x1, local copies, waits for them, and re-layouts  2.02 us

profile of v6, /device:TPU:1, one launch (start us, length us, event | category | flops | bytes accessed | tf_op | source)
XLA Modules:
  0.0 62.4 jit_solution(955003580069662382)
XLA Ops:
  0.0 60.4 %shard_map.82 = bf16[128,16384]{1,0:T(8,128)(2,1)S(1)} custom-call(bf16[128,16384]{1,0:T(8,128)(2,1)} %bitcast.3, bf16[512]{0:T(512)(128)(2,1)} %gain_hbm.1, bf16[512,256]{1,0:T(8,128)(2,1)} %wq.1, bf16[512,128]{1,0:T(8,128)(2,1)} %wk.1, bf16[512,128]{1,0:T(8,128)(2,1)} %wv.1, bf16[256,512]{1,0:T(8,128)(2,1)} %wo.1, s32[1,4]{1,0:T(1,128)} %dl_hbm.1, ...), custom_call_target="tpu_custom_call" | custom-call | tf_op jit(solution)/shard_map/pallas_call | solution.py:384
  60.4 2.0 %copy.10 = bf16[1,128,16384]{2,1,0:T(8,128)(2,1)} copy(bf16[1,128,16384]{2,1,0:T(8,128)(2,1)S(1)} %bitcast.2) | data formatting | bytes 8388608
